TPU v7x, 512 devices: a whole 4x4x16 slice. The times are simulated.
512 devices in a mesh: dp: 8 (over x, core), expert: 64 (over z, y).
Axes of the slice: x: 4, y: 4, z: 16, core: 2. Of those that a mesh axis runs over, the one named last changes fastest.
Arguments:
- grad_out: bfloat16 [65536, 2048], P(('dp', 'expert')), may hold values from -6 to 6
- gates: bfloat16 [65536, 6], P(('dp', 'expert')), may hold values from 0.049804688 to 0.59765625
- routes: int32 [65536, 6], P(('dp', 'expert')), may hold values from 0 to 63, all different within a row; in each aligned block of 128 rows (0 to 127, 128 to 255, ...) at most 16 rows name the same one
- hidden: bfloat16 [8, 64, 1024, 704], P('dp', 'expert'), may hold values from -0.23925781 to 0.23925781
- down_weight: bfloat16 [64, 704, 2048], P('expert', 'dp'), may hold values from -0.125 to 0.125
Outputs:
- grad_weight: bfloat16 [64, 704, 2048], P('expert', 'dp')
- grad_hidden: bfloat16 [8, 64, 1024, 704], P('dp', 'expert')
- grad_gates: float32 [65536, 6], P(('dp', 'expert'))
Inputs may be any that keep to these rules, and one draw needn't show every extreme that they name: `routes`: each row names 6 different experts; within the rows of one device no expert is named more than 16 times, a bound that some block reaches.
All inputs are finite; a program needn't handle non-finite values.
Results may differ from a plain program's by a relative error of at most 0.017.
Values may be sent and summed in bfloat16 or wider, within the bound.
A program may use at most 64 MiB of HBM per device.

v0:
```python
import jax
import jax.numpy as jnp
from jax import lax
from jax.sharding import PartitionSpec as P


def shards(grad_out, gates, routes, hidden, down_weight):
    owners = lax.axis_size("expert")
    token_count, chosen = routes.shape
    width = grad_out.shape[1]
    slots = hidden.shape[2]
    capacity = slots // owners
    flat = routes.reshape(-1)
    onehot = (flat[:, None] == jnp.arange(owners, dtype=jnp.int32)[None, :]).astype(jnp.int32)
    before = jnp.cumsum(onehot, axis=0) - onehot
    slot = jnp.sum(before * onehot, axis=1)
    target = flat * capacity + slot
    send_rows = (
        jnp.zeros((owners * capacity, width), grad_out.dtype)
        .at[target]
        .set(jnp.repeat(grad_out, chosen, axis=0))
    )
    send_gate = jnp.zeros((owners * capacity,), gates.dtype).at[target].set(gates.reshape(-1))
    send_rows = send_rows.reshape(owners, capacity, width)
    send_gate = send_gate.reshape(owners, capacity)
    saved = hidden[0, 0]
    local_weight = down_weight[0]
    contract = (((1,), (1,)), ((), ()))
    rows, gate_slots = (
        lax.all_to_all(send_rows, "expert", split_axis=0, concat_axis=0, tiled=True),
        lax.all_to_all(send_gate, "expert", split_axis=0, concat_axis=0, tiled=True),
    )
    rows = rows.reshape(slots, width)
    whole_weight = lax.all_gather(local_weight, "dp", axis=0, tiled=True)
    raw = lax.dot_general(rows, whole_weight, contract, preferred_element_type=jnp.float32)
    factor = gate_slots.reshape(slots, 1).astype(jnp.float32)
    grad_hidden = (factor * raw).astype(jnp.bfloat16)
    slot_grads = jnp.sum(raw * saved.astype(jnp.float32), axis=1)
    returned = lax.all_to_all(
        slot_grads.reshape(owners, capacity), "expert", split_axis=0, concat_axis=0, tiled=True
    )
    grad_gates = returned.reshape(-1)[target].reshape(token_count, chosen)
    scaled = (factor * rows.astype(jnp.float32)).astype(jnp.bfloat16)
    summed = lax.psum_scatter(
        lax.dot_general(
            saved, scaled, (((0,), (0,)), ((), ())), preferred_element_type=jnp.float32
        ).astype(jnp.bfloat16),
        "dp",
        scatter_dimension=0,
        tiled=True,
    )
    return (summed[None], grad_hidden[None, None], grad_gates)


def solution(mesh):
    return jax.shard_map(
        shards,
        mesh=mesh,
        in_specs=(
            P(("dp", "expert"), None),
            P(("dp", "expert"), None),
            P(("dp", "expert"), None),
            P("dp", "expert", None, None),
            P("expert", "dp", None),
        ),
        out_specs=(
            P("expert", "dp", None),
            P("dp", "expert", None, None),
            P(("dp", "expert"), None),
        ),
        check_vma=False,
    )
```

profile of v0, /device:TPU:1, one launch (start us, length us, event | category | flops | bytes accessed | tf_op | source)
XLA Modules:
  0.0 311.8 jit_solution(10308750628744932744)
XLA Ops:
  7.2 0.8 copy.15
  8.0 0.1 eq.29
  8.1 0.1 eq.25
  8.2 0.7 broadcast_multiply_fusion
  8.9 1.8 reduce-window.6
  10.7 0.3 slice_reduce_fusion
  11.1 0.1 copy.14
  11.2 0.1 mul.41
  11.3 0.8 copy.18
  12.1 0.1 reshape.120
  12.3 0.1 fusion.9
  12.4 8.6 %scatter_custom_fusion = bf16[1024]{0:T(1024)(128)(2,1)S(1)} fusion(s32[768]{0:T(1024)S(1)} %fusion.11, bf16[768]{0:T(1024)(128)(2,1)S(1)} %reshape.120, bf16[]{:T(256)} %constant.5.clone.1), kind=kCustom, calls=%fused_computation.27 | custom fusion | bytes 2050 | tf_op jit(solution)/shard_map/scatter | solution.py:23
  21.1 0.7 all_to_all.20
  21.8 19.3 %all-to-all-start = ((bf16[64,1,16]{2,1,0:T(2,128)(2,1)}), bf16[64,1,16]{2,1,0:T(2,128)(2,1)S(1)}, u32[]{:S(2)}, u32[]{:S(2)}) async-start(bf16[64,1,16]{2,1,0:T(2,128)(2,1)} %all_to_all.20), calls=%async_computation | async-start | bytes 65536 | tf_op jit(solution)/shard_map/all_to_all | solution.py:31
  41.0 3.6 %broadcast_in_dim.21 = bf16[128,6,2048]{2,1,0:T(8,128)(2,1)} broadcast(bf16[128,2048]{1,0:T(8,128)(2,1)} %param.5), dimensions={0,2} | broadcast | bytes 3670016 | tf_op jit(solution)/shard_map/broadcast_in_dim | solution.py:21
  44.7 4.9 %reshape.128 = bf16[768,2048]{1,0:T(8,128)(2,1)S(1)} reshape(bf16[128,6,2048]{2,1,0:T(8,128)(2,1)} %broadcast_in_dim.21) | data formatting | bytes 6291456 | tf_op jit(solution)/shard_map/reshape | solution.py:21
  49.6 9.4 %scatter_custom_fusion.1 = bf16[1024,2048]{1,0:T(8,128)(2,1)} fusion(s32[768]{0:T(1024)S(1)} %fusion.11, bf16[768,2048]{1,0:T(8,128)(2,1)S(1)} %reshape.128, bf16[]{:T(256)} %constant.5.clone.1), kind=kCustom, calls=%fused_computation.10 | custom fusion | bytes 4194306 | tf_op jit(solution)/shard_map/scatter | solution.py:21
  59.0 14.8 %all-to-all-start.1 = ((bf16[64,16,2048]{2,1,0:T(8,128)(2,1)}), bf16[64,16,2048]{2,1,0:T(8,128)(2,1)}, u32[]{:S(2)}, u32[]{:S(2)}) async-start(bf16[64,16,2048]{2,1,0:T(8,128)(2,1)} %bitcast.41), calls=%async_computation.1 | async-start | bytes 8388608 | tf_op jit(solution)/shard_map/all_to_all | solution.py:30
  73.8 0.7 all-gather.3.cloned.1.call-update
  74.6 182.8 %all-to-all-done.1 = bf16[64,16,2048]{2,1,0:T(8,128)(2,1)} async-done(((bf16[64,16,2048]{2,1,0:T(8,128)(2,1)}), bf16[64,16,2048]{2,1,0:T(8,128)(2,1)}, u32[]{:S(2)}, u32[]{:S(2)}) %all-to-all-start.1) | async-done | bytes 4194336 | tf_op jit(solution)/shard_map/all_to_all | solution.py:30
  257.4 3.0 multiply_convert_fusion
  260.4 4.5 %fusion = bf16[704,2048]{1,0:T(8,128)(2,1)} fusion(bf16[1024,2048]{1,0:T(8,128)(2,1)S(1)} %bitcast.42, bf16[1,1,1024,704]{2,3,1,0:T(8,128)(2,1)S(1)} %copy-done), kind=kOutput, calls=%fused_computation.5 | convolution fusion | flops 2954231808 | bytes 8519680 | tf_op jit(solution)/shard_map/dot_general | solution.py:45
  265.1 7.4 %multiply_reduce_fusion = (f32[1024]{0:T(1024)S(1)}, bf16[1,1,1024,704]{2,3,1,0:T(8,128)(2,1)}) fusion(bf16[1,1,1024,704]{2,3,1,0:T(8,128)(2,1)S(1)} %copy-done, f32[1024]{0:T(1024)S(1)} %reshape.107, bf16[1024,2048]{1,0:T(8,128)(2,1)} %bitcast.7, bf16[1,704,2048]{2,1,0:T(8,128)(2,1)} %all-gather.3.cloned.1.call-done), kind=kOutput, calls=%fused_computation.8 | convolution fusion | flops 2956393472 | bytes 9969664 | tf_op jit(solution)/shard_map/dot_general | solution.py:35
  272.6 0.7 all_to_all.18
  273.2 11.4 %all-to-all-start.2 = ((f32[64,1,16]{2,1,0:T(1,128)}), f32[64,1,16]{2,1,0:T(1,128)S(1)}, u32[]{:S(2)}, u32[]{:S(2)}) async-start(f32[64,1,16]{2,1,0:T(1,128)} %bitcast.10), calls=%async_computation.3 | async-start | bytes 65536 | tf_op jit(solution)/shard_map/all_to_all | solution.py:39
  284.7 13.6 %all-to-all-done.2 = f32[64,1,16]{2,1,0:T(1,128)S(1)} async-done(((f32[64,1,16]{2,1,0:T(1,128)}), f32[64,1,16]{2,1,0:T(1,128)S(1)}, u32[]{:S(2)}, u32[]{:S(2)}) %all-to-all-start.2) | async-done | bytes 4128 | tf_op jit(solution)/shard_map/all_to_all | solution.py:39
  298.3 0.5 broadcast.65
  298.8 0.7 reduce.11
  299.6 3.2 %gather_fusion = f32[768]{0:T(1024)S(1)} fusion(f32[1024]{0:T(1024)S(1)} %reshape.104, s32[1024]{0:T(1024)S(1)} %pad_clamp_fusion), kind=kCustom, calls=%fused_computation | custom fusion | bytes 9216 | tf_op jit(solution)/shard_map/gather | solution.py:42
  302.8 0.1 reshape.105
  302.9 0.7 copy.21
  303.6 1.4 reduce-scatter.2.cloned.1.call-done
  (15 shorter events, 0.4 us)
Async XLA Ops:
  21.8 37.2 %all-to-all-start = ((bf16[64,1,16]{2,1,0:T(2,128)(2,1)}), bf16[64,1,16]{2,1,0:T(2,128)(2,1)S(1)}, u32[]{:S(2)}, u32[]{:S(2)}) async-start(bf16[64,1,16]{2,1,0:T(2,128)(2,1)} %all_to_all.20), calls=%async_computation | async-start | bytes 65536 | tf_op jit(solution)/shard_map/all_to_all | solution.py:31
  59.0 198.4 %all-to-all-start.1 = ((bf16[64,16,2048]{2,1,0:T(8,128)(2,1)}), bf16[64,16,2048]{2,1,0:T(8,128)(2,1)}, u32[]{:S(2)}, u32[]{:S(2)}) async-start(bf16[64,16,2048]{2,1,0:T(8,128)(2,1)} %bitcast.41), calls=%async_computation.1 | async-start | bytes 8388608 | tf_op jit(solution)/shard_map/all_to_all | solution.py:30
  73.8 191.4 %all-gather.3.cloned.1.call-start = ((), (), s32[]{:S(2)}) async-start(), calls=%async_computation.5 | async-start | bytes 3244032 | tf_op jit(solution)/shard_map/all_gather | solution.py:34
  74.5 230.5 %reduce-scatter.2.cloned.1.call-start = ((), (), s32[]{:S(2)}) async-start(), calls=%async_computation.4 | async-start | bytes 3244032 | tf_op jit(solution)/shard_map/reduce_scatter | solution.py:44
  257.4 3.1 copy-start
  273.2 25.1 %all-to-all-start.2 = ((f32[64,1,16]{2,1,0:T(1,128)}), f32[64,1,16]{2,1,0:T(1,128)S(1)}, u32[]{:S(2)}, u32[]{:S(2)}) async-start(f32[64,1,16]{2,1,0:T(1,128)} %bitcast.10), calls=%async_computation.3 | async-start | bytes 65536 | tf_op jit(solution)/shard_map/all_to_all | solution.py:39
Sparse Core Ops, SparseCore 0:
  76.7 36.2 all-gather.2
  265.1 39.8 reduce-scatter.1
where the time goes:
time: 313 us; the launch traced here: 312 us
  waiting for transfers between devices  198 us (63%)
  starting transfers between devices  45.6 us (15%)
  local copies, waits for them, and re-layouts  35.1 us (11%)
  between operations  14.2 us (5%)
  matrix products  11.9 us (4%)
  other arithmetic  6.57 us (2%)
    all_to_all x1, waiting for transfers between devices, shards(): lax.all_to_all(send_rows, 'expert', split_axis=0, concat_axis=0, tiled=True)  183 us
    all_to_all x1, starting transfers between devices, shards(): lax.all_to_all(send_gate, 'expert', split_axis=0, concat_axis=0, tiled=True)  19.3 us
    all_to_all x1, starting transfers between devices, shards(): lax.all_to_all(send_rows, 'expert', split_axis=0, concat_axis=0, tiled=True)  14.8 us
    all_to_all x1, waiting for transfers between devices, shards(): lax.all_to_all(slot_grads.reshape(owners, capacity), 'expert', split_axis...  13.6 us
    all_to_all x1, starting transfers between devices, shards(): lax.all_to_all(slot_grads.reshape(owners, capacity), 'expert', split_axis...  11.4 us
    scatter x1, local copies, waits for them, and re-layouts, shards(): send_rows = jnp.zeros((owners * capacity, width), grad_out.dtype).at[targ...  9.4 us
    scatter x1, local copies, waits for them, and re-layouts, shards(): jnp.zeros((owners * capacity,), gates.dtype).at[target]  8.61 us
    dot_general x1, matrix products, shards(): lax.dot_general(rows, whole_weight, contract, preferred_element_type=jnp....  7.43 us
  transfers between devices with their start and end apart: 5, of which 3 were waited for; matrix products, arithmetic and copies ran while one was open for 12% of the time, Pallas kernels for 0%

commit v1 on v0

v1 whole, which is shorter than its diff:
```python
import jax
import jax.numpy as jnp
from jax import lax
from jax.sharding import PartitionSpec as P

NY = 4


def shards(grad_out, gates, routes, hidden, down_weight):
    owners = lax.axis_size("expert")
    token_count, chosen = routes.shape
    width = grad_out.shape[1]
    slots = hidden.shape[2]
    capacity = slots // owners
    nz = owners // NY
    columns = [[z * NY + y for z in range(nz)] for y in range(NY)]
    slabs = [[z * NY + y for y in range(NY)] for z in range(nz)]
    me = lax.axis_index("expert")
    my_y = me % NY
    my_z = me // NY

    earlier = (
        jnp.arange(token_count)[:, None] < jnp.arange(token_count)[None, :]
    ).astype(jnp.bfloat16)
    both = jnp.concatenate([routes.astype(jnp.float32), gates.astype(jnp.float32)], axis=1).T
    every = lax.all_gather(both, "expert", axis=0)
    tokens = lax.all_gather(grad_out, "expert", axis=0, axis_index_groups=columns)
    whole_weight = lax.all_gather(down_weight[0], "dp", axis=0, tiled=True)

    column = lax.dynamic_index_in_dim(
        every.reshape(nz, NY, 2 * chosen, token_count), my_y, 1, keepdims=False
    )[:, :chosen]
    named = (my_z * NY + jnp.arange(NY)).astype(jnp.float32)
    hit = jnp.any(column[:, None] == named[None, :, None, None], axis=2)
    rank = jnp.einsum(
        "sqt,tu->squ", hit.astype(jnp.bfloat16), earlier, preferred_element_type=jnp.float32
    )
    places = jnp.arange(capacity, dtype=jnp.float32)
    select = (hit[:, :, None] & (rank[:, :, None] == places[None, None, :, None])).astype(
        jnp.bfloat16
    )
    picked = jnp.einsum(
        "sct,std->scd",
        select.reshape(nz, NY * capacity, token_count),
        tokens,
        preferred_element_type=jnp.float32,
    ).astype(jnp.bfloat16)
    rows = lax.all_to_all(
        picked.reshape(nz, NY, capacity, width),
        "expert",
        split_axis=1,
        concat_axis=1,
        tiled=True,
        axis_index_groups=slabs,
    ).reshape(slots, width)

    same = every[:, :chosen] == me.astype(jnp.float32)
    mine = jnp.any(same, axis=1)
    gate_of = jnp.sum(jnp.where(same, every[:, chosen:], 0.0), axis=1)
    place = jnp.dot(mine.astype(jnp.bfloat16), earlier, preferred_element_type=jnp.float32)
    factor = jnp.sum(
        jnp.where(
            mine[:, None] & (place[:, None] == places[None, :, None]), gate_of[:, None], 0.0
        ),
        axis=2,
    ).reshape(slots, 1)

    saved = hidden[0, 0]
    contract = (((1,), (1,)), ((), ()))
    raw = lax.dot_general(rows, whole_weight, contract, preferred_element_type=jnp.float32)
    grad_hidden = (factor * raw).astype(jnp.bfloat16)
    slot_grads = jnp.sum(raw * saved.astype(jnp.float32), axis=1)
    returned = lax.all_to_all(
        slot_grads.reshape(owners, capacity), "expert", split_axis=0, concat_axis=0, tiled=True
    )
    wanted = routes[:, :, None] == jnp.arange(owners, dtype=jnp.int32)
    own = jnp.any(wanted, axis=1)
    own_rank = jnp.dot(earlier.T, own.astype(jnp.bfloat16), preferred_element_type=jnp.float32)
    slot = jnp.sum(jnp.where(wanted, own_rank[:, None], 0.0), axis=2).astype(jnp.int32)
    grad_gates = returned.reshape(-1)[routes * capacity + slot]
    scaled = (factor * rows.astype(jnp.float32)).astype(jnp.bfloat16)
    summed = lax.psum_scatter(
        lax.dot_general(
            saved, scaled, (((0,), (0,)), ((), ())), preferred_element_type=jnp.float32
        ).astype(jnp.bfloat16),
        "dp",
        scatter_dimension=0,
        tiled=True,
    )
    return (summed[None], grad_hidden[None, None], grad_gates)


def solution(mesh):
    return jax.shard_map(
        shards,
        mesh=mesh,
        in_specs=(
            P(("dp", "expert"), None),
            P(("dp", "expert"), None),
            P(("dp", "expert"), None),
            P("dp", "expert", None, None),
            P("expert", "dp", None),
        ),
        out_specs=(
            P("expert", "dp", None),
            P("dp", "expert", None, None),
            P(("dp", "expert"), None),
        ),
        check_vma=False,
    )
```

time: 313 us -> 242 us (0.77)
  waiting for transfers between devices: 198 us -> 80 us
  blocking collectives: 0 us -> 94.2 us
  starting transfers between devices: 45.6 us -> 15 us
  local copies, waits for them, and re-layouts: 35.1 us -> 12.9 us
  matrix products: 11.9 us -> 17 us
    all_to_all x2 -> x1, waiting for transfers between devices: 183 us -> 47.5 us  [shards(): lax.all_to_all(picked.reshape(nz, NY, capacity, width), 'expert', split_a...]
    all_gather x0 -> x1, blocking collectives: none -> 94.2 us  [shards(): every = lax.all_gather(both, 'expert', axis=0)]
    all_to_all x2 -> x1, starting transfers between devices: 34.1 us -> 4.86 us  [shards(): lax.all_to_all(picked.reshape(nz, NY, capacity, width), 'expert', split_a...]
    scatter x2 -> x0, local copies, waits for them, and re-layouts: 18 us -> none  [the longest x1 9.4 us: shards(): send_rows = jnp.zeros((owners * capacity, width), grad_out.dtype).at[targ...]
    all_gather x1 -> x2, waiting for transfers between devices: 0.01 us -> 17.5 us  [the longest x1 17.5 us: shards(): lax.all_gather(grad_out, 'expert', axis=0, axis_index_groups=columns)]
    dot_general x0 -> x4, matrix products: none -> 5.03 us  [the longest x1 4.62 us: shards(): jnp.einsum('sct,std->scd', select.reshape(nz, NY * capacity, token_count)...]
    all_to_all x1, local copies, waits for them, and re-layouts: 0.7 us -> 4.75 us  [shards(): lax.all_to_all(picked.reshape(nz, NY, capacity, width), 'expert', split_a...]
    broadcast_in_dim x1, local copies, waits for them, and re-layouts: 3.64 us -> 0.13 us  [shards(): grad_gates = returned.reshape(-1)[routes * capacity + slot]]
  transfers between devices with their start and end apart: 5 -> 5, of which waited for: 3 -> 3; matrix products, arithmetic and copies ran while one was open for 12% -> 15% of each run, Pallas kernels for 0% -> 0%
where the time goes in v1:
time: 242 us; the launch traced here: 240 us
  blocking collectives  94.2 us (39%)
  waiting for transfers between devices  80 us (33%)
  matrix products  17 us (7%)
  starting transfers between devices  15 us (6%)
  between operations  13.9 us (6%)
  local copies, waits for them, and re-layouts  12.9 us (5%)
  other arithmetic  7.4 us (3%)
    all_gather x1, blocking collectives, shards(): every = lax.all_gather(both, 'expert', axis=0)  94.2 us
    all_to_all x1, waiting for transfers between devices, shards(): lax.all_to_all(picked.reshape(nz, NY, capacity, width), 'expert', split_a...  47.5 us
    all_gather x1, waiting for transfers between devices, shards(): lax.all_gather(grad_out, 'expert', axis=0, axis_index_groups=columns)  17.5 us
    all_to_all x1, waiting for transfers between devices, shards(): lax.all_to_all(slot_grads.reshape(owners, capacity), 'expert', split_axis...  13.6 us
    all_to_all x1, starting transfers between devices, shards(): lax.all_to_all(slot_grads.reshape(owners, capacity), 'expert', split_axis...  9.99 us
    dot_general x1, matrix products, shards(): lax.dot_general(rows, whole_weight, contract, preferred_element_type=jnp....  7.43 us
    all_to_all x1, starting transfers between devices, shards(): lax.all_to_all(picked.reshape(nz, NY, capacity, width), 'expert', split_a...  4.86 us
  transfers between devices with their start and end apart: 5, of which 3 were waited for; matrix products, arithmetic and copies ran while one was open for 15% of the time, Pallas kernels for 0%

profile of v1, /device:TPU:1, one launch (start us, length us, event | category | flops | bytes accessed | tf_op | source)
XLA Modules:
  0.0 240.4 jit_solution(2975409668360160233)
XLA Ops:
  7.2 0.7 all-gather.7.cloned.1.call-update
  7.9 0.7 all-gather.9.cloned.1.call-update
  8.7 0.7 convert_element_type.50
  9.4 0.7 fusion.8
  10.1 0.1 fusion.9
  10.2 0.7 select_reduce_fusion.1
  10.9 0.8 compare_select_fusion
  11.7 94.2 %all-gather.3 = f32[64,12,128]{2,1,0:T(8,128)S(1)} all-gather(f32[1,12,128]{2,1,0:T(8,128)S(1)} %maximum_bitcast_fusion), channel_id=2, replica_groups=mesh['dp'=8,'expert'=64] {'expert'}, dimensions={0}, use_global_device_ids=true | all-gather | bytes 399360 | tf_op jit(solution)/shard_map/all_gather | solution.py:26
  105.9 0.1 copy.53
  106.3 0.1 fusion.12
  106.5 0.2 fusion.6
  106.7 17.5 %all-gather.7.cloned.1.call-done = bf16[2048,2048]{1,0:T(8,128)(2,1)} async-done(((bf16[128,2048]{1,0:T(8,128)(2,1)}), bf16[2048,2048]{1,0:T(8,128)(2,1)}) %all-gather.7.cloned.1.call-update) | async-done | bytes 8388624 | tf_op jit(solution)/shard_map/all_gather | solution.py:27
  124.2 4.6 %convolution_convert_fusion = bf16[16,64,2048]{2,1,0:T(8,128)(2,1)S(1)} fusion(pred[16,64,128]{2,1,0:T(32,128)(4,1)S(1)} %fusion.6, bf16[16,128,2048]{2,1,0:T(8,128)(2,1)} %bitcast.43), kind=kOutput, calls=%fused_computation.2 | convolution fusion | flops 538968064 | bytes 12713984 | tf_op jit(solution)/shard_map/sct,std->scd/dot_general | solution.py:42
  128.9 2.3 copy.56
  131.1 4.9 %all-to-all-start = ((bf16[16,4,16,2048]{3,2,0,1:T(8,128)(2,1)}), bf16[16,4,16,2048]{3,2,0,1:T(8,128)(2,1)}, u32[]{:S(2)}, u32[]{:S(2)}) async-start(bf16[16,4,16,2048]{3,2,0,1:T(8,128)(2,1)} %copy.56), calls=%async_computation | async-start | bytes 8388608 | tf_op jit(solution)/shard_map/all_to_all | solution.py:48
  136.2 0.1 fusion.7
  136.3 0.1 fusion.11
  136.4 0.2 select_reduce_fusion
  136.7 47.5 %all-to-all-done = bf16[16,4,16,2048]{3,2,0,1:T(8,128)(2,1)} async-done(((bf16[16,4,16,2048]{3,2,0,1:T(8,128)(2,1)}), bf16[16,4,16,2048]{3,2,0,1:T(8,128)(2,1)}, u32[]{:S(2)}, u32[]{:S(2)}) %all-to-all-start) | async-done | bytes 4194336 | tf_op jit(solution)/shard_map/all_to_all | solution.py:48
  184.1 3.0 %multiply_convert_fusion = bf16[16,4,16,2048]{3,2,1,0:T(8,128)(2,1)S(1)} fusion(f32[16,4,16]{2,1,0:T(4,128)S(1)} %bitcast.47, bf16[16,4,16,2048]{3,2,0,1:T(8,128)(2,1)} %all-to-all-done), kind=kLoop, calls=%fused_computation.1 | loop fusion | flops 6291456 | bytes 8392704 | tf_op jit(solution)/shard_map/convert_element_type | solution.py:81
  187.2 4.5 %fusion = bf16[704,2048]{1,0:T(8,128)(2,1)} fusion(bf16[1024,2048]{1,0:T(8,128)(2,1)S(1)} %bitcast.45, bf16[1,1,1024,704]{2,3,1,0:T(8,128)(2,1)S(1)} %copy-done), kind=kOutput, calls=%fused_computation.4 | convolution fusion | flops 2954231808 | bytes 8519680 | tf_op jit(solution)/shard_map/dot_general | solution.py:83
  191.9 0.1 reshape.54
  192.1 4.7 %copy.57 = bf16[16,4,16,2048]{3,2,1,0:T(8,128)(2,1)} copy(bf16[16,4,16,2048]{3,2,0,1:T(8,128)(2,1)} %all-to-all-done) | data formatting | bytes 8388608 | tf_op jit(solution)/shard_map/all_to_all | solution.py:48
  196.8 7.4 %multiply_reduce_fusion = (f32[1024]{0:T(1024)S(1)}, bf16[1,1,1024,704]{2,3,1,0:T(8,128)(2,1)}) fusion(bf16[1,1,1024,704]{2,3,1,0:T(8,128)(2,1)S(1)} %copy-done, f32[1024]{0:T(1024)S(1)} %mul.37, bf16[1024,2048]{1,0:T(8,128)(2,1)} %bitcast.44, bf16[1,704,2048]{2,1,0:T(8,128)(2,1)} %all-gather.9.cloned.1.call-done), kind=kOutput, calls=%fused_computation.7 | convolution fusion | flops 2956393472 | bytes 9969664 | tf_op jit(solution)/shard_map/dot_general | solution.py:70
  204.2 0.7 all_to_all.10
  204.9 10.0 %all-to-all-start.1 = ((f32[64,1,16]{2,1,0:T(1,128)}), f32[64,1,16]{2,1,0:T(1,128)S(1)}, u32[]{:S(2)}, u32[]{:S(2)}) async-start(f32[64,1,16]{2,1,0:T(1,128)} %bitcast.17), calls=%async_computation.2 | async-start | bytes 65536 | tf_op jit(solution)/shard_map/all_to_all | solution.py:73
  214.9 13.6 %all-to-all-done.1 = f32[64,1,16]{2,1,0:T(1,128)S(1)} async-done(((f32[64,1,16]{2,1,0:T(1,128)}), f32[64,1,16]{2,1,0:T(1,128)S(1)}, u32[]{:S(2)}, u32[]{:S(2)}) %all-to-all-start.1) | async-done | bytes 4128 | tf_op jit(solution)/shard_map/all_to_all | solution.py:73
  228.5 0.5 broadcast.27
  229.1 0.7 reduce.3
  229.9 3.2 %gather_fusion = f32[768]{0:T(1024)S(1)} fusion(f32[1024]{0:T(1024)S(1)} %reshape.51, s32[1024]{0:T(1024)S(1)} %pad_clamp_fusion), kind=kCustom, calls=%fused_computation | custom fusion | bytes 9216 | tf_op jit(solution)/shard_map/gather | solution.py:80
  233.1 0.1 reshape.53
  233.2 0.7 copy.61
  (22 shorter events, 0.9 us)
Async XLA Ops:
  7.2 117.1 %all-gather.7.cloned.1.call-start = ((), (), s32[]{:S(2)}) async-start(), calls=%async_computation.4 | async-start | bytes 8912896 | tf_op jit(solution)/shard_map/all_gather | solution.py:27
  7.9 188.9 %all-gather.9.cloned.1.call-start = ((), (), s32[]{:S(2)}) async-start(), calls=%async_computation.5 | async-start | bytes 3244032 | tf_op jit(solution)/shard_map/all_gather | solution.py:28
  131.1 53.0 %all-to-all-start = ((bf16[16,4,16,2048]{3,2,0,1:T(8,128)(2,1)}), bf16[16,4,16,2048]{3,2,0,1:T(8,128)(2,1)}, u32[]{:S(2)}, u32[]{:S(2)}) async-start(bf16[16,4,16,2048]{3,2,0,1:T(8,128)(2,1)} %copy.56), calls=%async_computation | async-start | bytes 8388608 | tf_op jit(solution)/shard_map/all_to_all | solution.py:48
  136.0 97.9 %reduce-scatter.2.cloned.1.call-start = ((), (), s32[]{:S(2)}) async-start(), calls=%async_computation.3 | async-start | bytes 3244032 | tf_op jit(solution)/shard_map/reduce_scatter | solution.py:82
  184.1 3.1 %copy-start = (bf16[1,1,1024,704]{2,3,1,0:T(8,128)(2,1)S(1)}, bf16[1,1,1024,704]{2,3,1,0:T(8,128)(2,1)}, u32[]{:S(2)}) copy-start(bf16[1,1,1024,704]{2,3,1,0:T(8,128)(2,1)} %param.8) | copy-start | bytes 4325380
  204.9 23.6 %all-to-all-start.1 = ((f32[64,1,16]{2,1,0:T(1,128)}), f32[64,1,16]{2,1,0:T(1,128)S(1)}, u32[]{:S(2)}, u32[]{:S(2)}) async-start(f32[64,1,16]{2,1,0:T(1,128)} %bitcast.17), calls=%async_computation.2 | async-start | bytes 65536 | tf_op jit(solution)/shard_map/all_to_all | solution.py:73
Sparse Core Ops, SparseCore 0:
  10.1 114.1 all-gather.6
  126.3 32.6 all-gather.8
  191.9 38.4 reduce-scatter.1

commit v2 on v0

v2 whole, which is shorter than its diff:
```python
import functools

import jax
import jax.numpy as jnp
from jax import lax
from jax.experimental import pallas as pl
from jax.experimental.pallas import tpu as pltpu
from jax.sharding import PartitionSpec as P

NY = 4
LANES = 128


def travel(nz, top, tokens, meta, out, buf, mbuf, pick, up_s, up_r, dn_s, dn_r,
           mu_s, mu_r, md_s, md_r, ys, yr, ls):
    me = lax.axis_index("expert")
    y = lax.rem(me, NY)
    z = lax.div(me, NY)
    count, width = tokens.shape
    half = count // 2
    cap = out.shape[1] // NY
    reach = nz // 2

    def wrap(i):
        return lax.rem(i + nz, nz)

    above = wrap(z + 1) * NY + y
    below = wrap(z - 1) * NY + y

    barrier = pltpu.get_barrier_semaphore()
    for other in [above, below] + [z * NY + lax.rem(y + j, NY) for j in range(1, NY)]:
        pl.semaphore_signal(
            barrier, inc=1, device_id={"expert": other}, device_id_type=pl.DeviceIdType.MESH
        )
    pl.semaphore_wait(barrier, NY + 1)

    def remote(src, dst, send, recv, to):
        return pltpu.make_async_remote_copy(
            src_ref=src, dst_ref=dst, send_sem=send, recv_sem=recv,
            device_id={"expert": to}, device_id_type=pl.DeviceIdType.MESH,
        )

    def piece(ref, part):
        return ref.at[pl.ds(pl.multiple_of(part * half, half), half)]

    def up(n, first=False):
        src = wrap(z - lax.div(n, 2))
        dst = piece(buf.at[src], lax.rem(n, 2))
        own = piece(tokens, lax.rem(n, 2)) if first else dst
        return remote(own, dst, up_s.at[n], up_r.at[n], above)

    def up_in(n):
        src = wrap(z - 1 - lax.div(n, 2))
        dst = piece(buf.at[src], lax.rem(n, 2))
        return remote(dst, dst, up_s.at[n], up_r.at[n], above)

    def down(n, first=False):
        src = wrap(z + lax.div(n, 2))
        dst = piece(buf.at[src], 1 - lax.rem(n, 2))
        own = piece(tokens, 1 - lax.rem(n, 2)) if first else dst
        return remote(own, dst, dn_s.at[n], dn_r.at[n], below)

    def down_in(n):
        src = wrap(z + 1 + lax.div(n, 2))
        dst = piece(buf.at[src], 1 - lax.rem(n, 2))
        return remote(dst, dst, dn_s.at[n], dn_r.at[n], below)

    def meta_up(n, first=False):
        dst = mbuf.at[wrap(z - n)]
        return remote(meta if first else dst, dst, mu_s.at[n], mu_r.at[n], above)

    def meta_up_in(n):
        dst = mbuf.at[wrap(z - 1 - n)]
        return remote(dst, dst, mu_s.at[n], mu_r.at[n], above)

    def meta_down(n, first=False):
        dst = mbuf.at[wrap(z + n)]
        return remote(meta if first else dst, dst, md_s.at[n], md_r.at[n], below)

    def meta_down_in(n):
        dst = mbuf.at[wrap(z + 1 + n)]
        return remote(dst, dst, md_s.at[n], md_r.at[n], below)

    meta_up(0, True).start()
    meta_down(0, True).start()
    for n in range(2):
        up(n, True).start()
        down(n, True).start()

    earlier = (
        lax.broadcasted_iota(jnp.int32, (count, count), 0)
        < lax.broadcasted_iota(jnp.int32, (count, count), 1)
    ).astype(jnp.bfloat16)
    places = lax.broadcasted_iota(jnp.int32, (cap, count), 0).astype(jnp.float32)

    def process(src, block, info):
        info = info.astype(jnp.float32)
        names, weights = info[:top], info[8:8 + top]
        hits, parts, gates = [], [], []
        for q in range(NY):
            same = names == (z * NY + q).astype(jnp.float32)
            hits.append(jnp.sum(jnp.where(same, 1.0, 0.0), axis=0, keepdims=True))
            gates.append(jnp.sum(jnp.where(same, weights, 0.0), axis=0, keepdims=True))
        rank = jnp.dot(
            jnp.concatenate(hits + hits, axis=0).astype(jnp.bfloat16),
            earlier,
            preferred_element_type=jnp.float32,
        )
        for q in range(NY):
            taken = (places == rank[q:q + 1]) & (hits[q] > 0.5)
            parts.append(jnp.where(taken, 1.0, 0.0))
            gate = jnp.sum(jnp.where(taken, gates[q], 0.0), axis=1, keepdims=True)
            pick[src, q * cap:(q + 1) * cap, width:] = jnp.broadcast_to(
                gate, (cap, LANES)
            ).astype(jnp.bfloat16)
        select = jnp.concatenate(parts, axis=0).astype(jnp.bfloat16)
        step = min(512, width)
        for c in range(0, width, step):
            pick[src, :, c:c + step] = jnp.dot(
                select, block[:, c:c + step], preferred_element_type=jnp.float32
            ).astype(jnp.bfloat16)

    def rows_of(ref, src, q):
        return ref.at[src, pl.ds(pl.multiple_of(q * cap, cap), cap)]

    def hand(src, j):
        q = lax.rem(y + j, NY)
        return remote(
            rows_of(pick, src, q), rows_of(out, src, y), ys.at[src, j - 1], yr.at[src, j - 1],
            z * NY + q,
        )

    def hand_in(src, j):
        q = lax.rem(y - j + NY, NY)
        return remote(
            rows_of(pick, src, q), rows_of(out, src, q), ys.at[src, j - 1], yr.at[src, j - 1],
            z * NY + q,
        )

    def keep(src):
        return pltpu.make_async_copy(rows_of(pick, src, y), rows_of(out, src, y), ls.at[src])

    def send(src):
        for j in range(1, NY):
            hand(src, j).start()
        keep(src).start()

    process(z, tokens, meta[...])

    def step(p, carry):
        for n in (2 * p, 2 * p + 1):
            up_in(n).wait_recv()
            pl.when(n + 2 <= 2 * reach - 2)(lambda n=n: up(n + 2).start())
            down_in(n).wait_recv()
            pl.when(n + 2 <= 2 * reach - 2)(lambda n=n: down(n + 2).start())
        meta_up_in(p).wait_recv()
        meta_up(p + 1).start()
        meta_down_in(p).wait_recv()
        pl.when(p + 1 <= reach - 2)(lambda: meta_down(p + 1).start())
        send(wrap(z + p))
        lower, upper = wrap(z - 1 - p), wrap(z + 1 + p)
        process(lower, buf.at[lower], mbuf[lower])
        process(upper, buf.at[upper], mbuf[upper])
        send(lower)
        return carry

    lax.fori_loop(0, reach - 1, step, 0)
    send(wrap(z + reach - 1))
    last = 2 * reach - 2
    far = wrap(z + reach)
    up_in(last).wait_recv()
    down_in(last).wait_recv()
    meta_up_in(reach - 1).wait_recv()
    process(far, buf.at[far], mbuf[far])

    for n in range(2):
        up(n, True).wait_send()
        down(n, True).wait_send()
    meta_up(0, True).wait_send()
    meta_down(0, True).wait_send()

    def sent(n, carry):
        up(n).wait_send()
        down(n).wait_send()
        return carry

    lax.fori_loop(2, 2 * reach - 1, sent, 0)

    def meta_sent(n, carry):
        meta_up(n).wait_send()
        pl.when(n <= reach - 2)(lambda: meta_down(n).wait_send())
        return carry

    lax.fori_loop(1, reach, meta_sent, 0)
    send(far)

    def done(src, carry):
        for j in range(1, NY):
            hand(src, j).wait_send()
            hand_in(src, j).wait_recv()
        keep(src).wait()
        return carry

    lax.fori_loop(0, nz, done, 0)


def bring(tokens, meta, nz, cap, top, number):
    count, width = tokens.shape
    reach = nz // 2
    full = width + LANES
    dma = pltpu.SemaphoreType.DMA
    return pl.pallas_call(
        functools.partial(travel, nz, top),
        out_shape=jax.ShapeDtypeStruct((nz, NY * cap, full), jnp.bfloat16),
        in_specs=[pl.BlockSpec(memory_space=pltpu.VMEM)] * 2,
        out_specs=pl.BlockSpec(memory_space=pl.ANY),
        scratch_shapes=[
            pltpu.VMEM((nz, count, width), jnp.bfloat16),
            pltpu.VMEM((nz,) + meta.shape, jnp.bfloat16),
            pltpu.VMEM((nz, NY * cap, full), jnp.bfloat16),
            dma((2 * reach - 1,)),
            dma((2 * reach - 1,)),
            dma((2 * reach - 1,)),
            dma((2 * reach - 1,)),
            dma((reach,)),
            dma((reach,)),
            dma((reach,)),
            dma((reach,)),
            dma((nz, NY - 1)),
            dma((nz, NY - 1)),
            dma((nz,)),
        ],
        compiler_params=pltpu.CompilerParams(
            collective_id=number, has_side_effects=True, vmem_limit_bytes=32 * 1024 * 1024
        ),
        cost_estimate=pl.CostEstimate(
            flops=2 * nz * NY * cap * count * width,
            bytes_accessed=160 * count * width * 2,
            transcendentals=0,
        ),
        name="bring_rows",
    )(tokens, meta)


def shards(grad_out, gates, routes, hidden, down_weight):
    owners = lax.axis_size("expert")
    token_count, chosen = routes.shape
    width = grad_out.shape[1]
    slots = hidden.shape[2]
    capacity = slots // owners
    nz = owners // NY

    earlier = (
        jnp.arange(token_count)[:, None] < jnp.arange(token_count)[None, :]
    ).astype(jnp.bfloat16)
    pad = jnp.zeros((8 - chosen, token_count), jnp.bfloat16)
    meta = jnp.concatenate([routes.T.astype(jnp.bfloat16), pad, gates.T, pad], axis=0)
    whole_weight = lax.all_gather(down_weight[0], "dp", axis=0, tiled=True)
    found = bring(grad_out, meta, nz, capacity, chosen, 0).reshape(slots, width + LANES)
    rows = found[:, :width]
    factor = found[:, width:width + 1].astype(jnp.float32)

    saved = hidden[0, 0]
    contract = (((1,), (1,)), ((), ()))
    raw = lax.dot_general(rows, whole_weight, contract, preferred_element_type=jnp.float32)
    grad_hidden = (factor * raw).astype(jnp.bfloat16)
    slot_grads = jnp.sum(raw * saved.astype(jnp.float32), axis=1)
    returned = lax.all_to_all(
        slot_grads.reshape(owners, capacity), "expert", split_axis=0, concat_axis=0, tiled=True
    )
    wanted = routes[:, :, None] == jnp.arange(owners, dtype=jnp.int32)
    own = jnp.any(wanted, axis=1)
    own_rank = jnp.dot(earlier.T, own.astype(jnp.bfloat16), preferred_element_type=jnp.float32)
    slot = jnp.sum(jnp.where(wanted, own_rank[:, None], 0.0), axis=2).astype(jnp.int32)
    grad_gates = returned.reshape(-1)[routes * capacity + slot]
    scaled = (factor * rows.astype(jnp.float32)).astype(jnp.bfloat16)
    summed = lax.psum_scatter(
        lax.dot_general(
            saved, scaled, (((0,), (0,)), ((), ())), preferred_element_type=jnp.float32
        ).astype(jnp.bfloat16),
        "dp",
        scatter_dimension=0,
        tiled=True,
    )
    return (summed[None], grad_hidden[None, None], grad_gates)


def solution(mesh):
    return jax.shard_map(
        shards,
        mesh=mesh,
        in_specs=(
            P(("dp", "expert"), None),
            P(("dp", "expert"), None),
            P(("dp", "expert"), None),
            P("dp", "expert", None, None),
            P("expert", "dp", None),
        ),
        out_specs=(
            P("expert", "dp", None),
            P("dp", "expert", None, None),
            P(("dp", "expert"), None),
        ),
        check_vma=False,
    )
```

time: 313 us -> 175 us (0.56)
  waiting for transfers between devices: 198 us -> 17.4 us
  Pallas kernels: 0 us -> 106 us
  starting transfers between devices: 45.6 us -> 9.46 us
  local copies, waits for them, and re-layouts: 35.1 us -> 8.74 us
    all_to_all x2 -> x0, waiting for transfers between devices: 183 us -> none  [the longest x1 183 us: shards(): lax.all_to_all(send_rows, 'expert', split_axis=0, concat_axis=0, tiled=True)]
    pallas_call x0 -> x1, Pallas kernels: none -> 106 us  [bring(): pl.pallas_call(functools.partial(travel, nz, top), out_shape=jax.ShapeDty...]
    all_to_all x2 -> x0, starting transfers between devices: 34.1 us -> none  [the longest x1 19.3 us: shards(): lax.all_to_all(send_gate, 'expert', split_axis=0, concat_axis=0, tiled=True)]
    scatter x2 -> x0, local copies, waits for them, and re-layouts: 18 us -> none  [the longest x1 9.4 us: shards(): send_rows = jnp.zeros((owners * capacity, width), grad_out.dtype).at[targ...]
    reshape x4 -> x1, local copies, waits for them, and re-layouts: 5.22 us -> 0.08 us  [shards(): grad_gates = returned.reshape(-1)[routes * capacity + slot]]
    broadcast_in_dim x1 -> x2, local copies, waits for them, and re-layouts: 3.64 us -> 0.14 us  [the longest x1 0.13 us: shards(): grad_gates = returned.reshape(-1)[routes * capacity + slot]]
    convert_element_type x4 -> x0, other arithmetic: 3.18 us -> none  [the longest x1 3.04 us: shards(): scaled = (factor * rows.astype(jnp.float32)).astype(jnp.bfloat16)]
  transfers between devices with their start and end apart: 5 -> 3, of which waited for: 3 -> 2; matrix products, arithmetic and copies ran while one was open for 12% -> 13% of each run, Pallas kernels for 0% -> 61%
where the time goes in v2:
time: 175 us; the launch traced here: 174 us
  Pallas kernels  106 us (61%)
  waiting for transfers between devices  17.4 us (10%)
  matrix products  14.5 us (8%)
  between operations  14.1 us (8%)
  starting transfers between devices  9.46 us (5%)
  local copies, waits for them, and re-layouts  8.74 us (5%)
  other arithmetic  3.67 us (2%)
    pallas_call x1, Pallas kernels, bring(): pl.pallas_call(functools.partial(travel, nz, top), out_shape=jax.ShapeDty...  106 us
    all_to_all x1, waiting for transfers between devices, shards(): lax.all_to_all(slot_grads.reshape(owners, capacity), 'expert', split_axis...  13.6 us
    all_to_all x1, starting transfers between devices, shards(): lax.all_to_all(slot_grads.reshape(owners, capacity), 'expert', split_axis...  9.38 us
    dot_general x1, matrix products, shards(): lax.dot_general(rows, whole_weight, contract, preferred_element_type=jnp....  7.43 us
    dot_general x1, matrix products, shards(): lax.dot_general(saved, scaled, (((0,), (0,)), ((), ())), preferred_elemen...  6.91 us
    unnamed x8, local copies, waits for them, and re-layouts  3.92 us
  transfers between devices with their start and end apart: 3, of which 2 were waited for; matrix products, arithmetic and copies ran while one was open for 13% of the time, Pallas kernels for 61%

profile of v2, /device:TPU:1, one launch (start us, length us, event | category | flops | bytes accessed | tf_op | source)
XLA Modules:
  0.0 174.2 jit_solution(4422724027844299707)
XLA Ops:
  7.2 0.0 all-gather.3.cloned.1.call-start
  7.2 0.7 all-gather.3.cloned.1.call-update
  7.9 0.0 reduce-scatter.2.cloned.1.call-start
  7.9 0.7 fusion.10
  8.7 0.1 fusion.11
  8.8 0.7 select_reduce_fusion
  9.5 0.8 compare_select_fusion
  10.3 0.7 pad_maximum_fusion.meta
  11.0 0.0 copy-start.1
  11.0 1.0 copy-done.1
  12.0 0.0 copy-start.2
  12.0 106.3 %bring_rows.1 = bf16[16,64,2176]{2,1,0:T(8,128)(2,1)S(1)} custom-call(bf16[128,2048]{1,0:T(8,128)(2,1)S(1)} %copy-done.1, bf16[16,128]{1,0:T(8,128)(2,1)S(1)} %pad_maximum_fusion.meta), custom_call_target="tpu_custom_call" | custom-call | flops 536870912 | bytes 83886080 | tf_op jit(solution)/shard_map/bring_rows/pallas_call | solution.py:212
  118.4 0.0 copy-start
  118.4 2.0 %copy-done = bf16[16,64,2176]{2,1,0:T(8,128)(2,1)} copy-done((bf16[16,64,2176]{2,1,0:T(8,128)(2,1)}, bf16[16,64,2176]{2,1,0:T(8,128)(2,1)S(1)}, u32[]{:S(2)}) %copy-start) | copy-done | bytes 4456472
  120.4 0.2 copy.26
  120.6 0.0 copy-done.2
  120.6 6.9 %fusion.6 = bf16[704,2048]{1,0:T(8,128)(2,1)} fusion(f32[1024]{0:T(1024)S(1)} %bitcast.24, bf16[1024,2176]{1,0:T(8,128)(2,1)} %bitcast.22, bf16[1,1,1024,704]{2,3,1,0:T(8,128)(2,1)S(1)} %copy-done.2), kind=kOutput, calls=%fused_computation.8 | convolution fusion | flops 2960523264 | bytes 8523776 | tf_op jit(solution)/shard_map/dot_general | solution.py:278
  127.5 0.0 reduce-scatter.2.cloned.1.call-update
  127.6 0.1 copy.23
  127.7 0.1 reshape.24
  127.8 0.0 all-gather.3.cloned.1.call-done
  127.8 7.4 %multiply_reduce_fusion = (f32[1024]{0:T(1024)S(1)}, bf16[1,1,1024,704]{2,3,1,0:T(8,128)(2,1)}) fusion(bf16[1,1,1024,704]{2,3,1,0:T(8,128)(2,1)S(1)} %copy-done.2, f32[1024]{0:T(1024)S(1)} %bitcast.25, bf16[1,704,2048]{2,1,0:T(8,128)(2,1)} %all-gather.3.cloned.1.call-done, bf16[1024,2176]{1,0:T(8,128)(2,1)} %bitcast.23), kind=kOutput, calls=%fused_computation.10 | convolution fusion | flops 2956393472 | bytes 9969664 | tf_op jit(solution)/shard_map/dot_general | solution.py:265
  135.3 0.7 all_to_all.6
  135.9 9.4 %all-to-all-start = ((f32[64,1,16]{2,1,0:T(1,128)}), f32[64,1,16]{2,1,0:T(1,128)S(1)}, u32[]{:S(2)}, u32[]{:S(2)}) async-start(f32[64,1,16]{2,1,0:T(1,128)} %bitcast.9), calls=%async_computation.1 | async-start | bytes 65536 | tf_op jit(solution)/shard_map/all_to_all | solution.py:268
  145.3 13.6 %all-to-all-done = f32[64,1,16]{2,1,0:T(1,128)S(1)} async-done(((f32[64,1,16]{2,1,0:T(1,128)}), f32[64,1,16]{2,1,0:T(1,128)S(1)}, u32[]{:S(2)}, u32[]{:S(2)}) %all-to-all-start) | async-done | bytes 4128 | tf_op jit(solution)/shard_map/all_to_all | solution.py:268
  159.0 0.5 broadcast.9
  159.5 0.7 reduce.3
  160.2 0.1 reshape.20
  160.3 3.2 %gather_fusion = f32[768]{0:T(1024)S(1)} fusion(f32[1024]{0:T(1024)S(1)} %reshape.20, s32[1024]{0:T(1024)S(1)} %pad_clamp_fusion), kind=kCustom, calls=%fused_computation | custom fusion | bytes 9216 | tf_op jit(solution)/shard_map/gather | solution.py:275
  163.5 0.1 reshape.23
  163.6 0.7 copy.24
  164.3 3.1 %reduce-scatter.2.cloned.1.call-done = bf16[88,2048]{1,0:T(8,128)(2,1)} async-done(((bf16[704,2048]{1,0:T(8,128)(2,1)}), bf16[88,2048]{1,0:T(8,128)(2,1)}) %reduce-scatter.2.cloned.1.call-update) | async-done | bytes 360464 | tf_op jit(solution)/shard_map/reduce_scatter | solution.py:277
  (3 shorter events, 0.0 us)
Async XLA Ops:
  7.2 120.7 %all-gather.3.cloned.1.call-start = ((), (), s32[]{:S(2)}) async-start(), calls=%async_computation.3 | async-start | bytes 3244032 | tf_op jit(solution)/shard_map/all_gather | solution.py:258
  7.9 159.5 %reduce-scatter.2.cloned.1.call-start = ((), (), s32[]{:S(2)}) async-start(), calls=%async_computation.2 | async-start | bytes 3244032 | tf_op jit(solution)/shard_map/reduce_scatter | solution.py:277
  11.0 1.0 copy-start.1
  12.0 108.6 %copy-start.2 = (bf16[1,1,1024,704]{2,3,1,0:T(8,128)(2,1)S(1)}, bf16[1,1,1024,704]{2,3,1,0:T(8,128)(2,1)}, u32[]{:S(2)}) copy-start(bf16[1,1,1024,704]{2,3,1,0:T(8,128)(2,1)} %param.8) | copy-start | bytes 4325380
  118.4 2.0 %copy-start = (bf16[16,64,2176]{2,1,0:T(8,128)(2,1)}, bf16[16,64,2176]{2,1,0:T(8,128)(2,1)S(1)}, u32[]{:S(2)}) copy-start(bf16[16,64,2176]{2,1,0:T(8,128)(2,1)S(1)} %bring_rows.1) | copy-start | bytes 13369348
  135.9 23.0 %all-to-all-start = ((f32[64,1,16]{2,1,0:T(1,128)}), f32[64,1,16]{2,1,0:T(1,128)S(1)}, u32[]{:S(2)}, u32[]{:S(2)}) async-start(f32[64,1,16]{2,1,0:T(1,128)} %bitcast.9), calls=%async_computation.1 | async-start | bytes 65536 | tf_op jit(solution)/shard_map/all_to_all | solution.py:268
Sparse Core Ops, SparseCore 0:
  10.1 39.9 all-gather.2
  127.7 39.6 reduce-scatter.1

commit v3 on v0

v3 whole, which is shorter than its diff:
```python
import functools

import jax
import jax.numpy as jnp
from jax import lax
from jax.experimental import pallas as pl
from jax.experimental.pallas import tpu as pltpu
from jax.sharding import PartitionSpec as P

NY = 4
LANES = 128


PASSES = 2
UNIT = 256
PAD = 8


def whole(nz, n_dp, top, tokens, meta, shard, saved, gw, gh, gg, buf, mbuf, pick, sel, rows,
          wall, wpad, savedp, savedg, raw, gate, partial, rs_in, sg, col, ret,
          up_s, up_r, dn_s, dn_r, mu_s, mu_r, md_s, md_r, ys, yr, ls, ws, wr, gs, gr,
          cs, cr, zs, zr):
    me = lax.axis_index("expert")
    dp = lax.axis_index("dp")
    y = lax.rem(me, NY)
    z = lax.div(me, NY)
    count, width = tokens.shape
    cap = pick.shape[1] // NY
    slots = nz * NY * cap
    depth = shard.shape[0]
    tall = depth + PAD
    reach = nz // 2
    per = 2 * reach - 1
    span = width // PASSES
    part = span // 2
    f32, bf16 = jnp.float32, jnp.bfloat16

    def wrap(i):
        return lax.rem(i + nz, nz)

    above = {"expert": wrap(z + 1) * NY + y}
    below = {"expert": wrap(z - 1) * NY + y}
    mesh_id = pl.DeviceIdType.MESH

    barrier = pltpu.get_barrier_semaphore()
    greet = [above, below] + [{"expert": z * NY + lax.rem(y + j, NY)} for j in range(1, NY)]
    greet = greet + [{"dp": lax.rem(dp + j, n_dp)} for j in range(1, n_dp)]
    for other in greet:
        pl.semaphore_signal(barrier, inc=1, device_id=other, device_id_type=mesh_id)
    pl.semaphore_wait(barrier, len(greet))

    def remote(src, dst, send, recv, to):
        return pltpu.make_async_remote_copy(
            src_ref=src, dst_ref=dst, send_sem=send, recv_sem=recv,
            device_id=to, device_id_type=mesh_id,
        )

    def own_piece(p, h):
        return tokens.at[:, pl.ds(p * span + h * part, part)]

    def up(p, n, odd, first=False):
        dst = buf.at[wrap(z - lax.div(n, 2)), p * 2 + odd]
        g = p * per + n
        return remote(own_piece(p, odd) if first else dst, dst, up_s.at[g], up_r.at[g], above)

    def up_in(p, n, odd):
        dst = buf.at[wrap(z - 1 - lax.div(n, 2)), p * 2 + odd]
        g = p * per + n
        return remote(dst, dst, up_s.at[g], up_r.at[g], above)

    def down(p, n, odd, first=False):
        dst = buf.at[wrap(z + lax.div(n, 2)), p * 2 + 1 - odd]
        g = p * per + n
        return remote(own_piece(p, 1 - odd) if first else dst, dst, dn_s.at[g], dn_r.at[g], below)

    def down_in(p, n, odd):
        dst = buf.at[wrap(z + 1 + lax.div(n, 2)), p * 2 + 1 - odd]
        g = p * per + n
        return remote(dst, dst, dn_s.at[g], dn_r.at[g], below)

    def meta_up(n, first=False):
        dst = mbuf.at[wrap(z - n)]
        return remote(meta if first else dst, dst, mu_s.at[n], mu_r.at[n], above)

    def meta_up_in(n):
        dst = mbuf.at[wrap(z - 1 - n)]
        return remote(dst, dst, mu_s.at[n], mu_r.at[n], above)

    def meta_down(n, first=False):
        dst = mbuf.at[wrap(z + n)]
        return remote(meta if first else dst, dst, md_s.at[n], md_r.at[n], below)

    def meta_down_in(n):
        dst = mbuf.at[wrap(z + 1 + n)]
        return remote(dst, dst, md_s.at[n], md_r.at[n], below)

    meta_up(0, True).start()
    meta_down(0, True).start()
    for n in range(2):
        up(0, n, n, True).start()
        down(0, n, n, True).start()

    def spread(j):
        return remote(shard, wall.at[dp], ws.at[j], wr.at[j], {"dp": lax.rem(dp + j, n_dp)})

    def spread_in(j):
        return remote(shard, wall.at[lax.rem(dp - j + n_dp, n_dp)], ws.at[j], wr.at[j],
                      {"dp": lax.rem(dp + j, n_dp)})

    for j in range(1, n_dp):
        spread(j).start()

    earlier = (
        lax.broadcasted_iota(jnp.int32, (count, count), 0)
        < lax.broadcasted_iota(jnp.int32, (count, count), 1)
    ).astype(bf16)
    places = lax.broadcasted_iota(jnp.int32, (cap, count), 0).astype(f32)

    def cols(p):
        return (0 if p == 0 else LANES + p * span), LANES + (p + 1) * span

    def choose(src, info):
        info = info.astype(f32)
        names, weights = info[:top], info[8:8 + top]
        hits, parts, gates = [], [], []
        for q in range(NY):
            same = names == (z * NY + q).astype(f32)
            hits.append(jnp.sum(jnp.where(same, 1.0, 0.0), axis=0, keepdims=True))
            gates.append(jnp.sum(jnp.where(same, weights, 0.0), axis=0, keepdims=True))
        rank = jnp.dot(
            jnp.concatenate(hits + hits, axis=0).astype(bf16), earlier,
            preferred_element_type=f32,
        )
        for q in range(NY):
            taken = (places == rank[q:q + 1]) & (hits[q] > 0.5)
            parts.append(jnp.where(taken, 1.0, 0.0))
            one = jnp.sum(jnp.where(taken, gates[q], 0.0), axis=1, keepdims=True)
            pick[src, q * cap:(q + 1) * cap, :LANES] = jnp.broadcast_to(one, (cap, LANES)).astype(
                bf16
            )
        sel[src] = jnp.concatenate(parts, axis=0).astype(bf16)

    def process(p, src, info, mine=False):
        if p == 0:
            choose(src, info)
        chosen = sel[src]
        for h in range(2):
            a = p * span + h * part
            block = tokens[:, a:a + part] if mine else buf[src, p * 2 + h]
            pick[src, :, LANES + a:LANES + a + part] = jnp.dot(
                chosen, block, preferred_element_type=f32
            ).astype(bf16)

    def rows_of(ref, p, src, q):
        a, b = cols(p)
        return ref.at[src, pl.ds(pl.multiple_of(q * cap, cap), cap), pl.ds(a, b - a)]

    def hand(p, src, j):
        q = lax.rem(y + j, NY)
        return remote(rows_of(pick, p, src, q), rows_of(rows, p, src, y),
                      ys.at[p, src, j - 1], yr.at[p, src, j - 1], {"expert": z * NY + q})

    def hand_in(p, src, j):
        q = lax.rem(y - j + NY, NY)
        return remote(rows_of(pick, p, src, q), rows_of(rows, p, src, q),
                      ys.at[p, src, j - 1], yr.at[p, src, j - 1], {"expert": z * NY + q})

    def keep(p, src):
        return pltpu.make_async_copy(rows_of(pick, p, src, y), rows_of(rows, p, src, y),
                                     ls.at[p, src])

    def send(p, src):
        for j in range(1, NY):
            hand(p, src, j).start()
        keep(p, src).start()

    def arrived(p):
        def done(src, carry):
            for j in range(1, NY):
                hand_in(p, src, j).wait_recv()
            keep(p, src).wait()
            return carry

        lax.fori_loop(0, nz, done, 0)

    def ready():
        first = (lax.broadcasted_iota(jnp.int32, (8, LANES), 1) == 0).astype(bf16)
        factor = lax.dot_general(
            first, rows[:, :, :LANES].reshape(slots, LANES), (((1,), (1,)), ((), ())),
            preferred_element_type=f32,
        )
        gate[...] = factor
        for j in range(1, n_dp):
            spread_in(j).wait_recv()
        for d in range(n_dp):
            mine = saved[d]
            savedp[d * tall:d * tall + depth] = mine
            savedp[d * tall + depth:(d + 1) * tall] = jnp.zeros((PAD, slots), bf16)
            savedg[d * tall:d * tall + depth] = (mine.astype(f32) * factor[0:1]).astype(bf16)
            savedg[d * tall + depth:(d + 1) * tall] = jnp.zeros((PAD, slots), bf16)
            wpad[d * tall + depth:(d + 1) * tall] = jnp.zeros((PAD, width), bf16)

        for d in range(n_dp):
            block = jnp.where(dp == d, shard[...], wall[d])
            wpad[d * tall:d * tall + depth] = block

    def weigh(p, u):
        a = p * span + u * UNIT
        right = rows[:, :, LANES + a:LANES + a + UNIT].reshape(slots, UNIT)
        out = jnp.dot(savedg[...], right, preferred_element_type=f32)
        for d in range(n_dp):
            partial[d, :, a:a + UNIT] = out[d * tall:d * tall + depth].astype(bf16)

    def share(p, u, j):
        a = p * span + u * UNIT
        d = lax.rem(dp + j, n_dp)
        k = p * (span // UNIT) + u
        return remote(partial.at[d, :, pl.ds(a, UNIT)], rs_in.at[dp, :, pl.ds(a, UNIT)],
                      gs.at[k, j], gr.at[k, j], {"dp": d})

    def share_in(p, u, j):
        a = p * span + u * UNIT
        d = lax.rem(dp - j + n_dp, n_dp)
        k = p * (span // UNIT) + u
        return remote(partial.at[d, :, pl.ds(a, UNIT)], rs_in.at[d, :, pl.ds(a, UNIT)],
                      gs.at[k, j], gr.at[k, j], {"dp": d})

    def give(p, u):
        for j in range(1, n_dp):
            share(p, u, j).start()

    def multiply(p, u):
        a = p * span
        lanes = slice(u * UNIT, (u + 1) * UNIT)
        few = UNIT // (NY * cap)
        right = rows[u * few:(u + 1) * few, :, LANES + a:LANES + a + span].reshape(UNIT, span)
        out = lax.dot_general(
            wpad[:, a:a + span], right, (((1,), (1,)), ((), ())), preferred_element_type=f32
        )
        if p > 0:
            out = out + raw[:, lanes]
        if p < PASSES - 1:
            raw[:, lanes] = out
            return
        scaled = out * gate[0:1, lanes]
        for d in range(n_dp):
            gh[d, :, lanes] = scaled[d * tall:d * tall + depth].astype(bf16)
        line = jnp.sum(out * savedp[:, lanes].astype(f32), axis=0, keepdims=True)
        for g in range(UNIT // LANES):
            sg[u * (UNIT // LANES) + g] = line[:, g * LANES:(g + 1) * LANES]

    wide = span // UNIT
    long = slots // UNIT
    process(0, z, meta[...], True)

    for p in range(PASSES):
        if p > 0:
            process(p, z, None, True)

        def step(i, carry, p=p):
            n = 2 * i
            up_in(p, n, 0).wait_recv()
            up(p, n + 2, 0).start()
            down_in(p, n, 0).wait_recv()
            down(p, n + 2, 0).start()
            n = n + 1
            up_in(p, n, 1).wait_recv()
            pl.when(i < reach - 2)(lambda: up(p, n + 2, 1).start())
            down_in(p, n, 1).wait_recv()
            pl.when(i < reach - 2)(lambda: down(p, n + 2, 1).start())
            if p + 1 < PASSES:
                def follow():
                    up(p + 1, 0, 0, True).start()
                    down(p + 1, 0, 0, True).start()

                pl.when(i == reach - 2)(follow)
            if p == 0:
                meta_up_in(i).wait_recv()
                meta_up(i + 1).start()
                meta_down_in(i).wait_recv()
                pl.when(i + 1 <= reach - 2)(lambda: meta_down(i + 1).start())
            send(p, wrap(z + i))
            lower, upper = wrap(z - 1 - i), wrap(z + 1 + i)
            process(p, lower, mbuf[lower] if p == 0 else None)
            process(p, upper, mbuf[upper] if p == 0 else None)
            send(p, lower)
            if p > 0:
                def begin():
                    arrived(p - 1)
                    if p == 1:
                        ready()

                pl.when(i == 1)(begin)
                for u in range(max(wide, long)):
                    def unit(u=u):
                        if u < wide:
                            weigh(p - 1, u)
                        if 0 < u <= wide:
                            give(p - 1, u - 1)
                        if u < long:
                            multiply(p - 1, u)
                        if u == max(wide, long) - 1 and u < wide:
                            give(p - 1, u)

                    pl.when(i == 2 + u)(unit)
            return carry

        lax.fori_loop(0, reach - 1, step, 0)
        send(p, wrap(z + reach - 1))
        last = per - 1
        far = wrap(z + reach)
        up_in(p, last, 0).wait_recv()
        down_in(p, last, 0).wait_recv()
        if p + 1 < PASSES:
            up(p + 1, 1, 1, True).start()
            down(p + 1, 1, 1, True).start()
        if p == 0:
            meta_up_in(reach - 1).wait_recv()
        process(p, far, mbuf[far] if p == 0 else None)
        if p == PASSES - 1:
            for n in range(2):
                for k in range(PASSES):
                    up(k, n, n, True).wait_send()
                    down(k, n, n, True).wait_send()
        send(p, far)

    own = meta[...].astype(f32)[:top]
    owner = lax.broadcasted_iota(jnp.int32, (nz * NY, count), 0).astype(f32)
    chosen = [owner == own[k:k + 1] for k in range(top)]
    taken = jnp.where(chosen[0], 1.0, 0.0)
    for k in range(1, top):
        taken = taken + jnp.where(chosen[k], 1.0, 0.0)
    own_rank = jnp.dot(taken.astype(bf16), earlier, preferred_element_type=f32)
    slot = [jnp.sum(jnp.where(chosen[k], own_rank, 0.0), axis=0, keepdims=True) for k in range(top)]

    end = PASSES - 1
    arrived(end)
    for u in range(wide):
        weigh(end, u)
        if u > 0:
            give(end, u - 1)
    for u in range(long):
        multiply(end, u)
        if u == 0:
            give(end, wide - 1)

    def cross(j):
        return remote(sg, col.at[y], cs.at[j], cr.at[j], {"expert": z * NY + lax.rem(y + j, NY)})

    def cross_in(j):
        return remote(sg, col.at[lax.rem(y - j + NY, NY)], cs.at[j], cr.at[j],
                      {"expert": z * NY + lax.rem(y + j, NY)})

    def back(j):
        s = lax.rem(z + j, nz)
        return remote(col.at[:, lax.div(s, 2)], ret.at[z], zs.at[j], zr.at[j],
                      {"expert": s * NY + y})

    def back_in(j):
        s = lax.rem(z - j + nz, nz)
        return remote(col.at[:, lax.div(s, 2)], ret.at[s], zs.at[j], zr.at[j],
                      {"expert": s * NY + y})

    for j in range(1, NY):
        cross(j).start()
    col[y] = sg[...]
    for j in range(1, NY):
        cross_in(j).wait_recv()
    lax.fori_loop(1, nz, lambda j, c: (back(j).start(), c)[1], 0)
    ret[z] = col[:, lax.div(z, 2)]

    for p in range(PASSES):
        for u in range(wide):
            for j in range(1, n_dp):
                share_in(p, u, j).wait_recv()
            a = p * span + u * UNIT
            total = partial[dp, :, a:a + UNIT].astype(f32)
            for j in range(1, n_dp):
                total = total + rs_in[lax.rem(dp + j, n_dp), :, a:a + UNIT].astype(f32)
            gw[:, a:a + UNIT] = total.astype(bf16)

    lax.fori_loop(1, nz, lambda j, c: (back_in(j).wait_recv(), c)[1], 0)
    table = ret[...].reshape(nz * NY, LANES)
    base = (lax.rem(me, LANES // cap) * cap).astype(f32)
    line = lax.broadcasted_iota(jnp.int32, (LANES, count), 0).astype(f32)
    for k in range(top):
        values = lax.dot_general(
            table, jnp.where(chosen[k], 1.0, 0.0), (((0,), (0,)), ((), ())),
            preferred_element_type=f32, precision=lax.Precision.HIGHEST,
        )
        gg[k:k + 1] = jnp.sum(
            jnp.where(line == slot[k] + base, values, 0.0), axis=0, keepdims=True
        )

    for p in range(PASSES):
        def sent(i, carry, p=p):
            for odd in range(2):
                up(p, 2 * i + odd, odd).wait_send()
                down(p, 2 * i + odd, odd).wait_send()
            return carry

        lax.fori_loop(1, reach - 1, sent, 0)
        up(p, per - 1, 0).wait_send()
        down(p, per - 1, 0).wait_send()

        def handed(src, carry, p=p):
            for j in range(1, NY):
                hand(p, src, j).wait_send()
            return carry

        lax.fori_loop(0, nz, handed, 0)
        for u in range(wide):
            for j in range(1, n_dp):
                share(p, u, j).wait_send()

    meta_up(0, True).wait_send()
    meta_down(0, True).wait_send()

    def meta_sent(n, carry):
        meta_up(n).wait_send()
        pl.when(n <= reach - 2)(lambda: meta_down(n).wait_send())
        return carry

    lax.fori_loop(1, reach, meta_sent, 0)
    for j in range(1, n_dp):
        spread(j).wait_send()
    for j in range(1, NY):
        cross(j).wait_send()
    lax.fori_loop(1, nz, lambda j, c: (back(j).wait_send(), c)[1], 0)


def shards(grad_out, gates, routes, hidden, down_weight):
    owners = lax.axis_size("expert")
    n_dp = lax.axis_size("dp")
    count, top = routes.shape
    width = grad_out.shape[1]
    slots, units = hidden.shape[2:]
    cap = slots // owners
    depth = units // n_dp
    tall = depth + PAD
    nz = owners // NY
    reach = nz // 2
    per = 2 * reach - 1
    full = width + LANES
    f32, bf16 = jnp.float32, jnp.bfloat16

    pad = jnp.zeros((8 - top, count), bf16)
    meta = jnp.concatenate([routes.T.astype(bf16), pad, gates.T, pad], axis=0)
    saved = hidden[0, 0].T.reshape(n_dp, depth, slots)
    dma = pltpu.SemaphoreType.DMA
    ring = [dma((PASSES * per,))] * 4 + [dma((reach,))] * 4
    vmem = pl.BlockSpec(memory_space=pltpu.VMEM)
    shares = width // UNIT
    gw, gh, gg = pl.pallas_call(
        functools.partial(whole, nz, n_dp, top),
        out_shape=(
            jax.ShapeDtypeStruct((depth, width), bf16),
            jax.ShapeDtypeStruct((n_dp, depth, slots), bf16),
            jax.ShapeDtypeStruct((8, count), f32),
        ),
        in_specs=[vmem] * 4,
        out_specs=(vmem, vmem, vmem),
        scratch_shapes=[
            pltpu.VMEM((nz, 2 * PASSES, count, width // (2 * PASSES)), bf16),
            pltpu.VMEM((nz,) + meta.shape, bf16),
            pltpu.VMEM((nz, NY * cap, full), bf16),
            pltpu.VMEM((nz, NY * cap, count), bf16),
            pltpu.VMEM((nz, NY * cap, full), bf16),
            pltpu.VMEM((n_dp, depth, width), bf16),
            pltpu.VMEM((n_dp * tall, width), bf16),
            pltpu.VMEM((n_dp * tall, slots), bf16),
            pltpu.VMEM((n_dp * tall, slots), bf16),
            pltpu.VMEM((n_dp * tall, slots), f32),
            pltpu.VMEM((8, slots), f32),
            pltpu.VMEM((n_dp, depth, width), bf16),
            pltpu.VMEM((n_dp, depth, width), bf16),
            pltpu.VMEM((slots // LANES, 1, LANES), f32),
            pltpu.VMEM((NY, slots // LANES, 1, LANES), f32),
            pltpu.VMEM((nz, NY, 1, LANES), f32),
        ]
        + ring
        + [dma((PASSES, nz, NY - 1))] * 2
        + [dma((PASSES, nz))]
        + [dma((n_dp,))] * 2
        + [dma((shares, n_dp))] * 2
        + [dma((NY,))] * 2
        + [dma((nz,))] * 2,
        compiler_params=pltpu.CompilerParams(
            collective_id=0, has_side_effects=True, vmem_limit_bytes=60 * 1024 * 1024
        ),
        name="routed_backward",
    )(grad_out, meta, down_weight[0], saved)
    grad_hidden = gh.reshape(units, slots).T
    return gw[None], grad_hidden[None, None], gg[:top].T


def solution(mesh):
    return jax.shard_map(
        shards,
        mesh=mesh,
        in_specs=(
            P(("dp", "expert"), None),
            P(("dp", "expert"), None),
            P(("dp", "expert"), None),
            P("dp", "expert", None, None),
            P("expert", "dp", None),
        ),
        out_specs=(
            P("expert", "dp", None),
            P("dp", "expert", None, None),
            P(("dp", "expert"), None),
        ),
        check_vma=False,
    )
```

time: 313 us -> 141 us (0.45)
  waiting for transfers between devices: 198 us -> 0 us
  Pallas kernels: 0 us -> 132 us
  starting transfers between devices: 45.6 us -> 0 us
  local copies, waits for them, and re-layouts: 35.1 us -> 5.59 us
  between operations: 14.2 us -> 0.64 us
  matrix products: 11.9 us -> 0 us
  other arithmetic: 6.57 us -> 1.97 us
    all_to_all x3 -> x0, waiting for transfers between devices: 196 us -> none  [the longest x1 183 us: shards(): lax.all_to_all(send_rows, 'expert', split_axis=0, concat_axis=0, tiled=True)]
    pallas_call x0 -> x1, Pallas kernels: none -> 132 us  [shards(): pl.pallas_call(functools.partial(whole, nz, n_dp, top), out_shape=(jax.Sh...]
    all_to_all x3 -> x0, starting transfers between devices: 45.5 us -> none  [the longest x1 19.3 us: shards(): lax.all_to_all(send_gate, 'expert', split_axis=0, concat_axis=0, tiled=True)]
    scatter x2 -> x0, local copies, waits for them, and re-layouts: 18 us -> none  [the longest x1 9.4 us: shards(): send_rows = jnp.zeros((owners * capacity, width), grad_out.dtype).at[targ...]
    dot_general x2 -> x0, matrix products: 11.9 us -> none  [the longest x1 7.43 us: shards(): lax.dot_general(rows, whole_weight, contract, preferred_element_type=jnp....]
    reshape x4 -> x0, local copies, waits for them, and re-layouts: 5.22 us -> none  [the longest x1 4.87 us: shards(): jnp.repeat(grad_out, chosen, axis=0)]
    broadcast_in_dim x1, local copies, waits for them, and re-layouts: 3.64 us -> 0.01 us  [shards(): pad = jnp.zeros((8 - top, count), bf16)]
    gather x1 -> x0, local copies, waits for them, and re-layouts: 3.18 us -> none  [shards(): grad_gates = returned.reshape(-1)[target].reshape(token_count, chosen)]
  transfers between devices with their start and end apart: 5 -> 0, of which waited for: 3 -> 0; matrix products, arithmetic and copies ran while one was open for 12% -> 0% of each run, Pallas kernels for 0% -> 0%
where the time goes in v3:
time: 141 us; the launch traced here: 140 us
  Pallas kernels  132 us (94%)
  local copies, waits for them, and re-layouts  5.59 us (4%)
  other arithmetic  1.97 us (1%)
    pallas_call x1, Pallas kernels, shards(): pl.pallas_call(functools.partial(whole, nz, n_dp, top), out_shape=(jax.Sh...  132 us
    unnamed x2, local copies, waits for them, and re-layouts  4.31 us

profile of v3, /device:TPU:1, one launch (start us, length us, event | category | flops | bytes accessed | tf_op | source)
XLA Modules:
  0.0 140.4 jit_solution(3965870635854196277)
XLA Ops:
  0.6 0.7 convert_bitcast_fusion
  1.3 1.3 pad_maximum_fusion.meta
  2.6 132.2 %routed_backward.1 = (bf16[88,2048]{1,0:T(8,128)(2,1)}, bf16[8,88,1024]{2,1,0:T(8,128)(2,1)}, f32[8,128]{1,0:T(8,128)}) custom-call(bf16[128,2048]{1,0:T(8,128)(2,1)} %tokens.1, bf16[16,128]{1,0:T(8,128)(2,1)} %pad_maximum_fusion.meta, bf16[88,2048]{1,0:T(8,128)(2,1)} %bitcast.19, bf16[8,88,1024]{2,1,0:T(8,128)(2,1)} %bitcast.17), custom_call_target="tpu_custom_call" | custom-call | tf_op jit(solution)/shard_map/routed_backward/pallas_call | solution.py:454
  134.8 1.3 slice_bitcast_fusion
  136.1 1.7 %copy.10 = bf16[1,88,2048]{2,1,0:T(8,128)(2,1)} copy(bf16[1,88,2048]{2,1,0:T(8,128)(2,1)} %bitcast.20) | data formatting | bytes 720896
  137.9 2.6 %copy.11 = bf16[1,1,1024,704]{2,3,1,0:T(8,128)(2,1)} copy(bf16[1,1,1024,704]{2,3,1,0:T(8,128)(2,1)} %bitcast.18) | data formatting | bytes 2883584
  (1 shorter events, 0.0 us)

commit v4 on v3

--- a/solution.py
+++ b/solution.py
@@ -11,15 +11,19 @@
 LANES = 128
 
 
-PASSES = 2
+SPANS = (1280, 768)
+PASSES = len(SPANS)
+STARTS = tuple(sum(SPANS[:p]) for p in range(PASSES))
+CORES = 2
+TICKS = 5
 UNIT = 256
 PAD = 8
 
 
-def whole(nz, n_dp, top, tokens, meta, shard, saved, gw, gh, gg, buf, mbuf, pick, sel, rows,
-          wall, wpad, savedp, savedg, raw, gate, partial, rs_in, sg, col, ret,
+def whole(nz, n_dp, top, tokens, meta, shard, saved, gw, gh, gg, buf0, buf1, mbuf, pick, sel, rows,
+          wall, wpad, savedp, savedg, raw, gate, partial, pair_in, both, rs_in, sg, col, ret,
           up_s, up_r, dn_s, dn_r, mu_s, mu_r, md_s, md_r, ys, yr, ls, ws, wr, gs, gr,
-          cs, cr, zs, zr):
+          ps, pr, cs, cr, zs, zr):
     me = lax.axis_index("expert")
     dp = lax.axis_index("dp")
     y = lax.rem(me, NY)
@@ -31,8 +35,10 @@
     tall = depth + PAD
     reach = nz // 2
     per = 2 * reach - 1
-    span = width // PASSES
-    part = span // 2
+    bufs = (buf0, buf1)
+    nx = n_dp // CORES
+    core = lax.rem(dp, CORES)
+    x = lax.div(dp, CORES)
     f32, bf16 = jnp.float32, jnp.bfloat16
 
     def wrap(i):
@@ -56,25 +62,26 @@
         )
 
     def own_piece(p, h):
-        return tokens.at[:, pl.ds(p * span + h * part, part)]
+        part = SPANS[p] // 2
+        return tokens.at[:, pl.ds(pl.multiple_of(STARTS[p] + h * part, LANES), part)]
 
     def up(p, n, odd, first=False):
-        dst = buf.at[wrap(z - lax.div(n, 2)), p * 2 + odd]
+        dst = bufs[p].at[wrap(z - lax.div(n, 2)), odd]
         g = p * per + n
         return remote(own_piece(p, odd) if first else dst, dst, up_s.at[g], up_r.at[g], above)
 
     def up_in(p, n, odd):
-        dst = buf.at[wrap(z - 1 - lax.div(n, 2)), p * 2 + odd]
+        dst = bufs[p].at[wrap(z - 1 - lax.div(n, 2)), odd]
         g = p * per + n
         return remote(dst, dst, up_s.at[g], up_r.at[g], above)
 
     def down(p, n, odd, first=False):
-        dst = buf.at[wrap(z + lax.div(n, 2)), p * 2 + 1 - odd]
+        dst = bufs[p].at[wrap(z + lax.div(n, 2)), 1 - odd]
         g = p * per + n
         return remote(own_piece(p, 1 - odd) if first else dst, dst, dn_s.at[g], dn_r.at[g], below)
 
     def down_in(p, n, odd):
-        dst = buf.at[wrap(z + 1 + lax.div(n, 2)), p * 2 + 1 - odd]
+        dst = bufs[p].at[wrap(z + 1 + lax.div(n, 2)), 1 - odd]
         g = p * per + n
         return remote(dst, dst, dn_s.at[g], dn_r.at[g], below)
 
@@ -117,7 +124,7 @@
     places = lax.broadcasted_iota(jnp.int32, (cap, count), 0).astype(f32)
 
     def cols(p):
-        return (0 if p == 0 else LANES + p * span), LANES + (p + 1) * span
+        return (0 if p == 0 else LANES + STARTS[p]), LANES + STARTS[p] + SPANS[p]
 
     def choose(src, info):
         info = info.astype(f32)
@@ -144,9 +151,10 @@
         if p == 0:
             choose(src, info)
         chosen = sel[src]
+        part = SPANS[p] // 2
         for h in range(2):
-            a = p * span + h * part
-            block = tokens[:, a:a + part] if mine else buf[src, p * 2 + h]
+            a = STARTS[p] + h * part
+            block = tokens[:, a:a + part] if mine else bufs[p][src, h]
             pick[src, :, LANES + a:LANES + a + part] = jnp.dot(
                 chosen, block, preferred_element_type=f32
             ).astype(bf16)
@@ -182,6 +190,18 @@
             return carry
 
         lax.fori_loop(0, nz, done, 0)
+
+    def keep_saved():
+        for d in range(n_dp):
+            savedp[d * tall:d * tall + depth] = saved[d]
+            savedp[d * tall + depth:(d + 1) * tall] = jnp.zeros((PAD, slots), bf16)
+
+    def keep_weight():
+        for j in range(1, n_dp):
+            spread_in(j).wait_recv()
+        for d in range(n_dp):
+            wpad[d * tall:d * tall + depth] = jnp.where(dp == d, shard[...], wall[d])
+            wpad[d * tall + depth:(d + 1) * tall] = jnp.zeros((PAD, width), bf16)
 
     def ready():
         first = (lax.broadcasted_iota(jnp.int32, (8, LANES), 1) == 0).astype(bf16)
@@ -190,47 +210,62 @@
             preferred_element_type=f32,
         )
         gate[...] = factor
-        for j in range(1, n_dp):
-            spread_in(j).wait_recv()
         for d in range(n_dp):
-            mine = saved[d]
-            savedp[d * tall:d * tall + depth] = mine
-            savedp[d * tall + depth:(d + 1) * tall] = jnp.zeros((PAD, slots), bf16)
-            savedg[d * tall:d * tall + depth] = (mine.astype(f32) * factor[0:1]).astype(bf16)
-            savedg[d * tall + depth:(d + 1) * tall] = jnp.zeros((PAD, slots), bf16)
-            wpad[d * tall + depth:(d + 1) * tall] = jnp.zeros((PAD, width), bf16)
-
-        for d in range(n_dp):
-            block = jnp.where(dp == d, shard[...], wall[d])
-            wpad[d * tall:d * tall + depth] = block
+            at = slice(d * tall, (d + 1) * tall)
+            savedg[at] = (savedp[at].astype(f32) * factor[0:1]).astype(bf16)
 
     def weigh(p, u):
-        a = p * span + u * UNIT
+        a = STARTS[p] + u * UNIT
         right = rows[:, :, LANES + a:LANES + a + UNIT].reshape(slots, UNIT)
         out = jnp.dot(savedg[...], right, preferred_element_type=f32)
         for d in range(n_dp):
-            partial[d, :, a:a + UNIT] = out[d * tall:d * tall + depth].astype(bf16)
+            partial[d % CORES, d // CORES, :, a:a + UNIT] = out[
+                d * tall:d * tall + depth
+            ].astype(bf16)
+
+    def pair(p, u):
+        a = STARTS[p] + u * UNIT
+        k = a // UNIT
+        return remote(partial.at[1 - core, :, :, pl.ds(a, UNIT)], pair_in.at[:, :, pl.ds(a, UNIT)],
+                      ps.at[k], pr.at[k], {"dp": x * CORES + 1 - core})
+
+    def combine(p, u):
+        pair(p, u).wait_recv()
+        a = STARTS[p] + u * UNIT
+        both[:, :, a:a + UNIT] = (
+            partial[core, :, :, a:a + UNIT].astype(f32) + pair_in[:, :, a:a + UNIT].astype(f32)
+        ).astype(bf16)
 
     def share(p, u, j):
-        a = p * span + u * UNIT
-        d = lax.rem(dp + j, n_dp)
-        k = p * (span // UNIT) + u
-        return remote(partial.at[d, :, pl.ds(a, UNIT)], rs_in.at[dp, :, pl.ds(a, UNIT)],
-                      gs.at[k, j], gr.at[k, j], {"dp": d})
+        a = STARTS[p] + u * UNIT
+        k = a // UNIT
+        to = lax.rem(x + j, nx)
+        return remote(both.at[to, :, pl.ds(a, UNIT)], rs_in.at[x, :, pl.ds(a, UNIT)],
+                      gs.at[k, j], gr.at[k, j], {"dp": to * CORES + core})
 
     def share_in(p, u, j):
-        a = p * span + u * UNIT
-        d = lax.rem(dp - j + n_dp, n_dp)
-        k = p * (span // UNIT) + u
-        return remote(partial.at[d, :, pl.ds(a, UNIT)], rs_in.at[d, :, pl.ds(a, UNIT)],
-                      gs.at[k, j], gr.at[k, j], {"dp": d})
-
-    def give(p, u):
-        for j in range(1, n_dp):
-            share(p, u, j).start()
+        a = STARTS[p] + u * UNIT
+        k = a // UNIT
+        near = lax.rem(x - j + nx, nx)
+        return remote(both.at[near, :, pl.ds(a, UNIT)], rs_in.at[near, :, pl.ds(a, UNIT)],
+                      gs.at[k, j], gr.at[k, j], {"dp": near * CORES + core})
+
+    def tick(p, t):
+        units = SPANS[p] // UNIT
+        if t < units:
+            weigh(p, t)
+        if 0 <= t - 1 < units:
+            pair(p, t - 1).start()
+        if t < long:
+            multiply(p, t)
+        if 0 <= t - 2 < units:
+            combine(p, t - 2)
+        if 0 <= t - 3 < units:
+            for j in range(1, nx):
+                share(p, t - 3, j).start()
 
     def multiply(p, u):
-        a = p * span
+        a, span = STARTS[p], SPANS[p]
         lanes = slice(u * UNIT, (u + 1) * UNIT)
         few = UNIT // (NY * cap)
         right = rows[u * few:(u + 1) * few, :, LANES + a:LANES + a + span].reshape(UNIT, span)
@@ -249,7 +284,6 @@
         for g in range(UNIT // LANES):
             sg[u * (UNIT // LANES) + g] = line[:, g * LANES:(g + 1) * LANES]
 
-    wide = span // UNIT
     long = slots // UNIT
     process(0, z, meta[...], True)
 
@@ -290,23 +324,20 @@
                     if p == 1:
                         ready()
 
+                if p == 1:
+                    pl.when(i == 0)(keep_weight)
                 pl.when(i == 1)(begin)
-                for u in range(max(wide, long)):
-                    def unit(u=u):
-                        if u < wide:
-                            weigh(p - 1, u)
-                        if 0 < u <= wide:
-                            give(p - 1, u - 1)
-                        if u < long:
-                            multiply(p - 1, u)
-                        if u == max(wide, long) - 1 and u < wide:
-                            give(p - 1, u)
-
-                    pl.when(i == 2 + u)(unit)
+                for t in range(TICKS):
+                    pl.when(i == 2 + t)(lambda t=t: tick(p - 1, t))
+            else:
+                pl.when(i == 3)(keep_saved)
             return carry
 
         lax.fori_loop(0, reach - 1, step, 0)
         send(p, wrap(z + reach - 1))
+        if p > 0:
+            for t in range(TICKS, SPANS[p - 1] // UNIT + 3):
+                tick(p - 1, t)
         last = per - 1
         far = wrap(z + reach)
         up_in(p, last, 0).wait_recv()
@@ -335,14 +366,8 @@
 
     end = PASSES - 1
     arrived(end)
-    for u in range(wide):
-        weigh(end, u)
-        if u > 0:
-            give(end, u - 1)
-    for u in range(long):
-        multiply(end, u)
-        if u == 0:
-            give(end, wide - 1)
+    for t in range(long):
+        tick(end, t)
 
     def cross(j):
         return remote(sg, col.at[y], cs.at[j], cr.at[j], {"expert": z * NY + lax.rem(y + j, NY)})
@@ -364,20 +389,12 @@
     for j in range(1, NY):
         cross(j).start()
     col[y] = sg[...]
+    for t in range(long, SPANS[end] // UNIT + 3):
+        tick(end, t)
     for j in range(1, NY):
         cross_in(j).wait_recv()
     lax.fori_loop(1, nz, lambda j, c: (back(j).start(), c)[1], 0)
     ret[z] = col[:, lax.div(z, 2)]
-
-    for p in range(PASSES):
-        for u in range(wide):
-            for j in range(1, n_dp):
-                share_in(p, u, j).wait_recv()
-            a = p * span + u * UNIT
-            total = partial[dp, :, a:a + UNIT].astype(f32)
-            for j in range(1, n_dp):
-                total = total + rs_in[lax.rem(dp + j, n_dp), :, a:a + UNIT].astype(f32)
-            gw[:, a:a + UNIT] = total.astype(bf16)
 
     lax.fori_loop(1, nz, lambda j, c: (back_in(j).wait_recv(), c)[1], 0)
     table = ret[...].reshape(nz * NY, LANES)
@@ -393,6 +410,16 @@
         )
 
     for p in range(PASSES):
+        for u in range(SPANS[p] // UNIT):
+            for j in range(1, nx):
+                share_in(p, u, j).wait_recv()
+            a = STARTS[p] + u * UNIT
+            total = both[x, :, a:a + UNIT].astype(f32)
+            for j in range(1, nx):
+                total = total + rs_in[lax.rem(x + j, nx), :, a:a + UNIT].astype(f32)
+            gw[:, a:a + UNIT] = total.astype(bf16)
+
+    for p in range(PASSES):
         def sent(i, carry, p=p):
             for odd in range(2):
                 up(p, 2 * i + odd, odd).wait_send()
@@ -409,8 +436,9 @@
             return carry
 
         lax.fori_loop(0, nz, handed, 0)
-        for u in range(wide):
-            for j in range(1, n_dp):
+        for u in range(SPANS[p] // UNIT):
+            pair(p, u).wait_send()
+            for j in range(1, nx):
                 share(p, u, j).wait_send()
 
     meta_up(0, True).wait_send()
@@ -461,7 +489,8 @@
         in_specs=[vmem] * 4,
         out_specs=(vmem, vmem, vmem),
         scratch_shapes=[
-            pltpu.VMEM((nz, 2 * PASSES, count, width // (2 * PASSES)), bf16),
+            pltpu.VMEM((nz, 2, count, SPANS[0] // 2), bf16),
+            pltpu.VMEM((nz, 2, count, SPANS[1] // 2), bf16),
             pltpu.VMEM((nz,) + meta.shape, bf16),
             pltpu.VMEM((nz, NY * cap, full), bf16),
             pltpu.VMEM((nz, NY * cap, count), bf16),
@@ -472,8 +501,10 @@
             pltpu.VMEM((n_dp * tall, slots), bf16),
             pltpu.VMEM((n_dp * tall, slots), f32),
             pltpu.VMEM((8, slots), f32),
-            pltpu.VMEM((n_dp, depth, width), bf16),
-            pltpu.VMEM((n_dp, depth, width), bf16),
+            pltpu.VMEM((CORES, n_dp // CORES, depth, width), bf16),
+            pltpu.VMEM((n_dp // CORES, depth, width), bf16),
+            pltpu.VMEM((n_dp // CORES, depth, width), bf16),
+            pltpu.VMEM((n_dp // CORES, depth, width), bf16),
             pltpu.VMEM((slots // LANES, 1, LANES), f32),
             pltpu.VMEM((NY, slots // LANES, 1, LANES), f32),
             pltpu.VMEM((nz, NY, 1, LANES), f32),
@@ -483,10 +514,11 @@
         + [dma((PASSES, nz))]
         + [dma((n_dp,))] * 2
         + [dma((shares, n_dp))] * 2
+        + [dma((shares,))] * 2
         + [dma((NY,))] * 2
         + [dma((nz,))] * 2,
         compiler_params=pltpu.CompilerParams(
-            collective_id=0, has_side_effects=True, vmem_limit_bytes=60 * 1024 * 1024
+            collective_id=0, has_side_effects=True, vmem_limit_bytes=46 * 1024 * 1024
         ),
         name="routed_backward",
     )(grad_out, meta, down_weight[0], saved)

time: 141 us -> 138 us (0.979)
  Pallas kernels: 132 us -> 130 us
    pallas_call x1, Pallas kernels: 132 us -> 130 us  [shards(): pl.pallas_call(functools.partial(whole, nz, n_dp, top), out_shape=(jax.Sh...]
    unnamed x2 -> x8, local copies, waits for them, and re-layouts: 4.31 us -> 5.22 us
where the time goes in v4:
time: 138 us
  Pallas kernels  130 us (94%)
  local copies, waits for them, and re-layouts  5.82 us (4%)
    pallas_call x1, Pallas kernels, shards(): pl.pallas_call(functools.partial(whole, nz, n_dp, top), out_shape=(jax.Sh...  130 us
    unnamed x8, local copies, waits for them, and re-layouts  5.22 us

profile of v4, /device:TPU:1, one launch (start us, length us, event | category | flops | bytes accessed | tf_op | source)
XLA Modules:
  0.0 137.6 jit_solution(2827536281047085791)
XLA Ops:
  0.6 0.7 convert_bitcast_fusion
  1.3 0.7 pad_maximum_fusion.meta
  2.0 0.0 copy-start
  2.0 1.4 copy-done
  3.4 0.0 copy-start.1
  3.4 1.0 copy-done.1
  4.4 0.0 copy-start.2
  4.4 1.0 copy-done.2
  5.4 129.7 %routed_backward.1 = (bf16[88,2048]{1,0:T(8,128)(2,1)S(1)}, bf16[8,88,1024]{2,1,0:T(8,128)(2,1)S(1)}, f32[8,128]{1,0:T(8,128)S(1)}) custom-call(bf16[128,2048]{1,0:T(8,128)(2,1)S(1)} %copy-done.1, bf16[16,128]{1,0:T(8,128)(2,1)S(1)} %pad_maximum_fusion.meta, bf16[88,2048]{1,0:T(8,128)(2,1)S(1)} %bitcast.19, bf16[8,88,1024]{2,1,0:T(8,128)(2,1)S(1)} %bitcast.17), custom_call_target="tpu_custom_call" | custom-call | tf_op jit(solution)/shard_map/routed_backward/pallas_call | solution.py:482
  135.1 0.6 slice_bitcast_fusion
  135.7 0.7 copy.10
  136.5 1.1 copy.11
  (1 shorter events, 0.0 us)
Async XLA Ops:
  2.0 1.4 copy-start
  3.4 1.0 copy-start.1
  4.4 1.0 copy-start.2

commit v5 on v4

--- a/solution.py
+++ b/solution.py
@@ -21,9 +21,9 @@
 
 
 def whole(nz, n_dp, top, tokens, meta, shard, saved, gw, gh, gg, buf0, buf1, mbuf, pick, sel, rows,
-          wall, wpad, savedp, savedg, raw, gate, partial, pair_in, both, rs_in, sg, col, ret,
+          saved_in, wall, wpad, savedp, savedg, raw, gate, partial, pair_in, both, rs_in, sg, col, ret,
           up_s, up_r, dn_s, dn_r, mu_s, mu_r, md_s, md_r, ys, yr, ls, ws, wr, gs, gr,
-          ps, pr, cs, cr, zs, zr):
+          ps, pr, cs, cr, zs, zr, fs):
     me = lax.axis_index("expert")
     dp = lax.axis_index("dp")
     y = lax.rem(me, NY)
@@ -116,6 +116,8 @@
 
     for j in range(1, n_dp):
         spread(j).start()
+    pltpu.make_async_copy(saved, saved_in, fs.at[0]).start()
+    pltpu.make_async_copy(shard, wall.at[dp], fs.at[1]).start()
 
     earlier = (
         lax.broadcasted_iota(jnp.int32, (count, count), 0)
@@ -192,15 +194,17 @@
         lax.fori_loop(0, nz, done, 0)
 
     def keep_saved():
+        pltpu.make_async_copy(saved, saved_in, fs.at[0]).wait()
         for d in range(n_dp):
-            savedp[d * tall:d * tall + depth] = saved[d]
+            savedp[d * tall:d * tall + depth] = saved_in[d]
             savedp[d * tall + depth:(d + 1) * tall] = jnp.zeros((PAD, slots), bf16)
 
     def keep_weight():
+        pltpu.make_async_copy(shard, wall.at[dp], fs.at[1]).wait()
         for j in range(1, n_dp):
             spread_in(j).wait_recv()
         for d in range(n_dp):
-            wpad[d * tall:d * tall + depth] = jnp.where(dp == d, shard[...], wall[d])
+            wpad[d * tall:d * tall + depth] = wall[d]
             wpad[d * tall + depth:(d + 1) * tall] = jnp.zeros((PAD, width), bf16)
 
     def ready():
@@ -250,19 +254,20 @@
         return remote(both.at[near, :, pl.ds(a, UNIT)], rs_in.at[near, :, pl.ds(a, UNIT)],
                       gs.at[k, j], gr.at[k, j], {"dp": near * CORES + core})
 
+    def forward(p, t):
+        units = SPANS[p] // UNIT
+        if 0 <= t - 2 < units:
+            combine(p, t - 2)
+        if 0 <= t - 3 < units:
+            for j in range(1, nx):
+                share(p, t - 3, j).start()
+
     def tick(p, t):
         units = SPANS[p] // UNIT
         if t < units:
             weigh(p, t)
         if 0 <= t - 1 < units:
             pair(p, t - 1).start()
-        if t < long:
-            multiply(p, t)
-        if 0 <= t - 2 < units:
-            combine(p, t - 2)
-        if 0 <= t - 3 < units:
-            for j in range(1, nx):
-                share(p, t - 3, j).start()
 
     def multiply(p, u):
         a, span = STARTS[p], SPANS[p]
@@ -297,6 +302,24 @@
             up(p, n + 2, 0).start()
             down_in(p, n, 0).wait_recv()
             down(p, n + 2, 0).start()
+            if p == 0:
+                pl.when(i == 3)(keep_saved)
+            else:
+                def begin():
+                    arrived(p - 1)
+                    if p == 1:
+                        ready()
+
+                def between(t):
+                    if t < long:
+                        multiply(p - 1, t)
+                    forward(p - 1, t)
+
+                if p == 1:
+                    pl.when(i == 0)(keep_weight)
+                pl.when(i == 1)(begin)
+                for t in range(TICKS):
+                    pl.when(i == 2 + t)(lambda t=t: between(t))
             n = n + 1
             up_in(p, n, 1).wait_recv()
             pl.when(i < reach - 2)(lambda: up(p, n + 2, 1).start())
@@ -319,18 +342,8 @@
             process(p, upper, mbuf[upper] if p == 0 else None)
             send(p, lower)
             if p > 0:
-                def begin():
-                    arrived(p - 1)
-                    if p == 1:
-                        ready()
-
-                if p == 1:
-                    pl.when(i == 0)(keep_weight)
-                pl.when(i == 1)(begin)
                 for t in range(TICKS):
                     pl.when(i == 2 + t)(lambda t=t: tick(p - 1, t))
-            else:
-                pl.when(i == 3)(keep_saved)
             return carry
 
         lax.fori_loop(0, reach - 1, step, 0)
@@ -338,6 +351,7 @@
         if p > 0:
             for t in range(TICKS, SPANS[p - 1] // UNIT + 3):
                 tick(p - 1, t)
+                forward(p - 1, t)
         last = per - 1
         far = wrap(z + reach)
         up_in(p, last, 0).wait_recv()
@@ -367,7 +381,7 @@
     end = PASSES - 1
     arrived(end)
     for t in range(long):
-        tick(end, t)
+        multiply(end, t)
 
     def cross(j):
         return remote(sg, col.at[y], cs.at[j], cr.at[j], {"expert": z * NY + lax.rem(y + j, NY)})
@@ -389,12 +403,26 @@
     for j in range(1, NY):
         cross(j).start()
     col[y] = sg[...]
-    for t in range(long, SPANS[end] // UNIT + 3):
-        tick(end, t)
+    tick(end, 0)
+    tick(end, 1)
     for j in range(1, NY):
         cross_in(j).wait_recv()
     lax.fori_loop(1, nz, lambda j, c: (back(j).start(), c)[1], 0)
     ret[z] = col[:, lax.div(z, 2)]
+
+    for t in range(2, SPANS[end] // UNIT + 3):
+        tick(end, t)
+        forward(end, t)
+
+    for p in range(PASSES):
+        for u in range(SPANS[p] // UNIT):
+            for j in range(1, nx):
+                share_in(p, u, j).wait_recv()
+            a = STARTS[p] + u * UNIT
+            total = both[x, :, a:a + UNIT].astype(f32)
+            for j in range(1, nx):
+                total = total + rs_in[lax.rem(x + j, nx), :, a:a + UNIT].astype(f32)
+            gw[:, a:a + UNIT] = total.astype(bf16)
 
     lax.fori_loop(1, nz, lambda j, c: (back_in(j).wait_recv(), c)[1], 0)
     table = ret[...].reshape(nz * NY, LANES)
@@ -408,16 +436,6 @@
         gg[k:k + 1] = jnp.sum(
             jnp.where(line == slot[k] + base, values, 0.0), axis=0, keepdims=True
         )
-
-    for p in range(PASSES):
-        for u in range(SPANS[p] // UNIT):
-            for j in range(1, nx):
-                share_in(p, u, j).wait_recv()
-            a = STARTS[p] + u * UNIT
-            total = both[x, :, a:a + UNIT].astype(f32)
-            for j in range(1, nx):
-                total = total + rs_in[lax.rem(x + j, nx), :, a:a + UNIT].astype(f32)
-            gw[:, a:a + UNIT] = total.astype(bf16)
 
     for p in range(PASSES):
         def sent(i, carry, p=p):
@@ -486,7 +504,7 @@
             jax.ShapeDtypeStruct((n_dp, depth, slots), bf16),
             jax.ShapeDtypeStruct((8, count), f32),
         ),
-        in_specs=[vmem] * 4,
+        in_specs=[vmem] * 2 + [pl.BlockSpec(memory_space=pltpu.HBM)] * 2,
         out_specs=(vmem, vmem, vmem),
         scratch_shapes=[
             pltpu.VMEM((nz, 2, count, SPANS[0] // 2), bf16),
@@ -495,6 +513,7 @@
             pltpu.VMEM((nz, NY * cap, full), bf16),
             pltpu.VMEM((nz, NY * cap, count), bf16),
             pltpu.VMEM((nz, NY * cap, full), bf16),
+            pltpu.VMEM((n_dp, depth, slots), bf16),
             pltpu.VMEM((n_dp, depth, width), bf16),
             pltpu.VMEM((n_dp * tall, width), bf16),
             pltpu.VMEM((n_dp * tall, slots), bf16),
@@ -516,7 +535,8 @@
         + [dma((shares, n_dp))] * 2
         + [dma((shares,))] * 2
         + [dma((NY,))] * 2
-        + [dma((nz,))] * 2,
+        + [dma((nz,))] * 2
+        + [dma((2,))],
         compiler_params=pltpu.CompilerParams(
             collective_id=0, has_side_effects=True, vmem_limit_bytes=46 * 1024 * 1024
         ),

time: 138 us -> 139 us (level)
  no operation moved by 1% of the time
where the time goes in v5:
time: 139 us
  Pallas kernels  131 us (94%)
  local copies, waits for them, and re-layouts  5.82 us (4%)
    pallas_call x1, Pallas kernels, shards(): pl.pallas_call(functools.partial(whole, nz, n_dp, top), out_shape=(jax.Sh...  131 us
    unnamed x8, local copies, waits for them, and re-layouts  5.22 us

profile of v5, /device:TPU:1, one launch (start us, length us, event | category | flops | bytes accessed | tf_op | source)
XLA Modules:
  0.0 138.8 jit_solution(13211040459285743324)
XLA Ops:
  0.6 0.7 convert_bitcast_fusion
  1.3 0.7 pad_maximum_fusion.meta
  2.0 0.0 copy-start
  2.0 1.4 copy-done
  3.4 0.0 copy-start.1
  3.4 1.0 copy-done.1
  4.4 0.0 copy-start.2
  4.4 1.0 copy-done.2
  5.4 131.0 %routed_backward.1 = (bf16[88,2048]{1,0:T(8,128)(2,1)S(1)}, bf16[8,88,1024]{2,1,0:T(8,128)(2,1)S(1)}, f32[8,128]{1,0:T(8,128)S(1)}) custom-call(bf16[128,2048]{1,0:T(8,128)(2,1)S(1)} %copy-done.1, bf16[16,128]{1,0:T(8,128)(2,1)S(1)} %pad_maximum_fusion.meta, bf16[88,2048]{1,0:T(8,128)(2,1)S(1)} %bitcast.19, bf16[8,88,1024]{2,1,0:T(8,128)(2,1)S(1)} %bitcast.17), custom_call_target="tpu_custom_call" | custom-call | tf_op jit(solution)/shard_map/routed_backward/pallas_call | solution.py:500
  136.4 0.6 slice_bitcast_fusion
  137.0 0.7 copy.10
  137.7 1.1 copy.11
  (1 shorter events, 0.0 us)
Async XLA Ops:
  2.0 1.4 copy-start
  3.4 1.0 copy-start.1
  4.4 1.0 copy-start.2
